TPU v7x, 256 devices: a whole 4x4x8 slice. The times are simulated.
256 devices in a mesh: wall: 2 (over z_lo), plane: 128 (over x, y, z_hi, core).
Axes of the slice: x: 4, y: 4, z: 8 (z_hi: 4, z_lo: 2; z = z_hi * 2 + z_lo), core: 2. Of those that a mesh axis runs over, the one named last changes fastest.
Arguments:
- jacobian: float32 [3, 16, 16, 32, 128, 128], P(None, None, None, 'wall', 'plane'), as said below
- residual: float32 [16, 32, 128, 128], P(None, 'wall', 'plane')
- previous_update: float32 [16, 32, 128, 128], P(None, 'wall', 'plane'), may hold values from -6 to 6
- offline_coupling: float32 [4, 16, 32, 128, 128], P(None, None, 'wall', 'plane'), may hold values from 0.003 to 0.03
- wake_partner: int32 [128, 128], P('plane'), may hold values from 0 to 127, each once within a row
- line_length: int32 [128, 128], P('plane'), may hold values from 16 to 32
- bottom_flag: int32 [128, 128], P('plane'), may hold values 0 or 1
Outputs:
- update: float32 [16, 32, 128, 128], P(None, 'wall', 'plane')
Inputs may be any that keep to these rules, and one draw needn't show every extreme that they name: jacobian[2, :, :, k] is the transpose of jacobian[0, :, :, k + 1], every jacobian[1, :, :, k] is symmetric, and every row of a line's matrix is strictly diagonally dominant with a positive diagonal. `bottom_flag`: 1 where a column's first cell lies on the wake cut, 0 where it lies on the capsule wall. `wake_partner`: for a wake-cut column (i, j), the spanwise index of the column at station (i + 64) modulo 128, on the other branch of the cut, that lies beneath its first cell; each row is a permutation of 0 to 127.
All inputs are finite; a program needn't handle non-finite values. No bound on the sum of `bottom_flag` on one device may be relied on, other than what follows from the above.
Results may differ from a plain program's by a relative error of at most 0.0003.
Values sent between devices are 32-bit elements; how exact they have to be, the bound alone decides.
No kernel may reach another device: no remote copies, remote signals or barrier semaphores. Data moves between devices by JAX's collectives and lax.ppermute only.
A program may use at most 192 MiB of HBM per device.

v0:
```python
import jax
import jax.numpy as jnp
from jax import lax
from jax.sharding import PartitionSpec as P

precise = lax.Precision.HIGHEST


def with_halo(block, sides, width):
    for axis, dim in sides:
        count = lax.axis_size(axis)
        forward = [(i, i + 1) for i in range(count - 1)]
        backward = [(target, source) for source, target in forward]
        low = lax.ppermute(
            lax.slice_in_dim(block, block.shape[dim] - width, None, axis=dim), axis, forward
        )
        high = lax.ppermute(lax.slice_in_dim(block, 0, width, axis=dim), axis, backward)
        block = jnp.concatenate([low, block, high], axis=dim)
    return block


def from_behind(block, axis, distance):
    devices = range(lax.axis_size(axis))
    route = [(i - distance, i) for i in devices if i - distance in devices]
    return lax.ppermute(block, axis, route)


def product(left, right):
    return jnp.einsum("vwc,wuc->vuc", left, right, precision=precise)


def solve_block(matrix, given):
    extent = matrix.shape[0]
    augmented = jnp.concatenate([matrix, given], axis=1)
    for pivot in range(extent):
        pivot_row = augmented[pivot] / augmented[pivot, pivot][None, :]
        augmented = augmented - augmented[:, pivot][:, None, :] * pivot_row[None]
        augmented = augmented.at[pivot].set(pivot_row)
    return augmented[:, extent:]


def effective(lower, middle, upper, active_here, active_above, not_bottom):
    identity = jnp.eye(lower.shape[0], dtype=jnp.float32)[:, :, None, None]
    return (
        lower * (active_here * not_bottom)[None, None],
        middle * active_here[None, None] + identity * (1.0 - active_here)[None, None],
        upper * active_above[None, None],
    )


def eliminate(lower, middle, upper, source, block_in, vector_in, levels):
    extent = lower.shape[0]
    blocks = jnp.zeros(lower.shape, jnp.float32)
    vectors = jnp.zeros(source.shape, jnp.float32)

    def advance(level, state):
        block_prev, vector_prev, blocks, vectors = state
        below = lax.dynamic_index_in_dim(lower, level, 2, keepdims=False)
        centre = lax.dynamic_index_in_dim(middle, level, 2, keepdims=False)
        above = lax.dynamic_index_in_dim(upper, level, 2, keepdims=False)
        given = lax.dynamic_index_in_dim(source, level, 2, keepdims=False)
        schur = centre - product(below, block_prev)
        reduced = given - product(below, vector_prev)
        joined = solve_block(schur, jnp.concatenate([above, reduced], axis=1))
        block_next = joined[:, :extent]
        vector_next = joined[:, extent:]
        blocks = lax.dynamic_update_index_in_dim(blocks, block_next, level, 2)
        vectors = lax.dynamic_update_index_in_dim(vectors, vector_next, level, 2)
        return (block_next, vector_next, blocks, vectors)

    return lax.fori_loop(0, levels, advance, (block_in, vector_in, blocks, vectors))


def substitute(blocks, vectors, value_above, levels, result):

    def retreat(count, state):
        value_next, result = state
        level = levels - 1 - count
        block = lax.dynamic_index_in_dim(blocks, level, 2, keepdims=False)
        vector = lax.dynamic_index_in_dim(vectors, level, 2, keepdims=False)
        value = vector - product(block, value_next)
        result = lax.dynamic_update_index_in_dim(result, value, level, 2)
        return (value, result)

    return lax.fori_loop(0, levels, retreat, (value_above, result))


def per_device(
    jacobian, residual, previous_update, offline_coupling, wake_partner, line_length, bottom_flag
):
    unknowns = jacobian.shape[1]
    depth = jacobian.shape[3]
    stations = jacobian.shape[4]
    span = jacobian.shape[5]
    columns = stations * span
    wall_index = lax.axis_index("wall")
    plane_index = lax.axis_index("plane")
    planes = lax.axis_size("plane")
    padded = with_halo(previous_update, (("plane", 2),), 1)
    offline = (
        offline_coupling[0] * padded[:, :, :-2]
        + offline_coupling[1] * padded[:, :, 2:]
        + offline_coupling[2] * jnp.roll(previous_update, 1, axis=3)
        + offline_coupling[3] * jnp.roll(previous_update, -1, axis=3)
    )
    bottom_row = previous_update[:, 0]
    mirror_index = (plane_index + planes // 2) % planes
    whole = lax.all_gather(bottom_row, "plane", axis=1, tiled=True)
    facing = lax.dynamic_slice_in_dim(whole, mirror_index * stations, stations, 1)
    partner = jnp.take_along_axis(facing, wake_partner[None], axis=2)
    weight = bottom_flag.astype(jnp.float32) * (wall_index == 0).astype(jnp.float32)
    wake = (
        jnp.einsum("vwij,wij->vij", jacobian[0, :, :, 0], partner, precision=precise) * weight[None]
    )
    levels = wall_index * depth + jnp.arange(depth, dtype=jnp.int32)
    active = (levels[:, None, None] < line_length[None]).astype(jnp.float32)
    active_above = ((levels + 1)[:, None, None] < line_length[None]).astype(jnp.float32)
    not_bottom = (levels > 0).astype(jnp.float32)[:, None]
    source = residual + offline
    source = source.at[:, 0].add(-wake)
    source = (source * active[None]).reshape(unknowns, 1, depth, columns)
    blocks = jacobian.reshape(3, unknowns, unknowns, depth, columns)
    lower, middle, upper = effective(
        blocks[0],
        blocks[1],
        blocks[2],
        active.reshape(depth, columns),
        active_above.reshape(depth, columns),
        not_bottom,
    )
    empty_block = jnp.zeros((unknowns, unknowns, columns), jnp.float32)
    empty_vector = jnp.zeros((unknowns, 1, columns), jnp.float32)
    block_in = empty_block
    vector_in = empty_vector
    parts = eliminate(lower, middle, upper, source, block_in, vector_in, depth)
    handed = from_behind(
        jnp.concatenate([parts[2][:, :, depth - 1], parts[3][:, :, depth - 1]], axis=1), "wall", 1
    )
    block_in = handed[:, :unknowns]
    vector_in = handed[:, unknowns:]
    parts = eliminate(lower, middle, upper, source, block_in, vector_in, depth)
    value_above = empty_vector
    solved = substitute(
        parts[2], parts[3], value_above, depth, jnp.zeros(source.shape, jnp.float32)
    )
    value_above = from_behind(solved[1][:, :, 0], "wall", -1)
    solution = substitute(
        parts[2], parts[3], value_above, depth, jnp.zeros(source.shape, jnp.float32)
    )[1]
    return solution[:, 0].reshape(unknowns, depth, stations, span)


def solution(mesh):
    return jax.shard_map(
        per_device,
        mesh=mesh,
        in_specs=(
            P(None, None, None, "wall", "plane", None),
            P(None, "wall", "plane", None),
            P(None, "wall", "plane", None),
            P(None, None, "wall", "plane", None),
            P("plane", None),
            P("plane", None),
            P("plane", None),
        ),
        out_specs=P(None, "wall", "plane", None),
        check_vma=False,
    )
```

profile of v0, /device:TPU:6, one launch (start us, length us, event | category | flops | bytes accessed | tf_op | source)
XLA Modules:
  0.0 604.7 jit_solution(280235571044377390)
XLA Ops:
  9.4 10.4 %collective-permute-start.1 = (f32[16,16,1,128]{3,0,1,2:T(8,128)S(1)}, f32[16,16,1,128]{3,0,1,2:T(8,128)S(1)}, u32[]{:S(2)}, u32[]{:S(2)}) collective-permute-start(f32[16,16,1,128]{3,0,1,2:T(8,128)S(1)} %copy.131), channel_id=1, source_target_pairs={{1,0},{2,1},{3,2},{4,3},{5,4},{6,5},{7,6},{8,7},{9,8},{10,9},{11,1... | collective-permute-start | bytes 393224 | tf_op jit(solution)/shard_map/ppermute | solution.py:17
  26.4 8.3 %fusion.22 = (f32[1,16,16,16,1,128]{5,4,3,2,1,0:T(1,128)}, f32[1,16,16,16,1,128]{5,4,3,2,1,0:T(1,128)}, f32[1,16,16,16,1,128]{5,4,3,2,1,0:T(1,128)S(1)}) fusion(f32[3,16,16,16,1,128]{5,4,3,2,1,0:T(1,128)} %param.81), kind=kLoop, calls=%fused_computation.232 | loop fusion | bytes 12582912 | tf_op jit(solution)/shard_map/slice | solution.py:126
  34.7 12.0 %copy.215 = f32[1,16,16,16,1,128]{2,1,5,3,4,0:T(8,128)} copy(f32[1,16,16,16,1,128]{5,4,3,2,1,0:T(1,128)} %get-tuple-element.1768) | data formatting | bytes 4194304
  46.7 10.7 %copy.216 = f32[1,16,16,16,1,128]{2,1,5,3,4,0:T(8,128)} copy(f32[1,16,16,16,1,128]{5,4,3,2,1,0:T(1,128)S(1)} %get-tuple-element.1769) | data formatting | bytes 4194304
  57.4 4.3 fusion.11
  61.7 15.1 %fusion.10 = f32[16,16,16,128]{1,0,3,2:T(8,128)} fusion(f32[1,16,16,16,1,128]{2,1,5,3,4,0:T(8,128)} %copy.215, f32[16,128]{1,0:T(8,128)S(1)} %copy-done.3, f32[16,16]{1,0:T(8,128)S(1)} %fusion.20, f32[16,128]{1,0:T(8,128)S(1)} %get-tuple-element.1781), kind=kLoop, calls=%fused_computation.191 | loop fusion | flops 1572864 | bytes 4211712 | tf_op jit(solution)/shard_map/add | solution.py:46
  76.9 6.4 %bitcast_multiply_fusion.2 = f32[16,16,16,128]{1,0,3,2:T(8,128)} fusion(f32[1,16,16,16,1,128]{2,1,5,3,4,0:T(8,128)S(1)} %bitcast.632, f32[16,128]{1,0:T(8,128)S(1)} %copy-done.2), kind=kLoop, calls=%fused_computation.189 | loop fusion | flops 524288 | bytes 4202496 | tf_op jit(solution)/shard_map/mul | solution.py:45
  84.6 17.8 %all-gather.3.cloned.1.call-done = f32[16,128,1,128]{3,2,1,0:T(1,128)} async-done(((f32[16,1,1,128]{3,2,1,0:T(1,128)}), f32[16,128,1,128]{3,2,1,0:T(1,128)}) %all-gather.3.cloned.1.call-update) | async-done | bytes 1048592 | tf_op jit(solution)/shard_map/all_gather | solution.py:108
  104.1 185.2 %while.112 = (s32[]{:T(128)}, f32[16,16,128]{2,0,1:T(8,128)S(1)}, f32[16,1,128]{2,0,1:T(8,128)S(1)}, f32[16,16,16,128]{3,0,1,2:T(8,128)}, f32[16,1,16,128]{3,0,2...) while((s32[]{:T(128)}, f32[16,16,128]{2,0,1:T(8,128)S(1)}, ...), condition=%wide.region_1.2_spmd, body=%wide.region_0.1_spmd.sunk | while | flops 8890370 | bytes 15271725 | solution.py:71
  199.0 2.8 fusion.39
  291.8 3.4 collective-permute-done.2
  295.3 249.2 %while.113 = (s32[]{:T(128)}, f32[16,16,128]{2,0,1:T(8,128)S(1)}, f32[16,1,128]{2,0,1:T(8,128)S(1)}, f32[16,16,16,128]{3,2,1,0:T(8,128)}, f32[16,1,16,128]{3,0,2...) while((s32[]{:T(128)}, f32[16,16,128]{2,0,1:T(8,128)S(1)}, ...), condition=%wide.region_3.4_spmd, body=%wide.region_2.3_spmd.sunk | while | flops 8890370 | bytes 15926577 | solution.py:71
  306.3 4.5 dynamic_update_slice.80
  321.9 4.5 dynamic_update_slice.80
  337.4 4.5 dynamic_update_slice.80
  353.0 4.5 dynamic_update_slice.80
  368.5 4.5 dynamic_update_slice.80
  384.1 4.5 dynamic_update_slice.80
  399.6 4.5 dynamic_update_slice.80
  415.2 4.5 dynamic_update_slice.80
  422.0 2.8 fusion.43
  430.8 4.5 dynamic_update_slice.80
  446.4 4.5 dynamic_update_slice.80
  462.0 4.5 dynamic_update_slice.80
  477.6 4.5 dynamic_update_slice.80
  493.2 4.5 dynamic_update_slice.80
  508.8 4.5 dynamic_update_slice.80
  524.4 4.5 dynamic_update_slice.80
  540.0 4.5 dynamic_update_slice.80
  544.5 23.7 %while.115 = (s32[]{:T(128)}, f32[16,1,128]{2,0,1:T(8,128)S(1)}, f32[16,1,16,128]{3,2,1,0:T(8,128)S(1)}, f32[16,1,16,128]{3,0,2,1:T(8,128)S(1)}, f32[16,16,16,12...) while((s32[]{:T(128)}, f32[16,1,128]{2,0,1:T(8,128)S(1)}, ...), condition=%wide.region_5.6_spmd.clone, body=%wide.region_4.5_spmd.clone.sunk | while | flops 67591 | bytes 467105 | solution.py:85
  569.5 4.2 collective-permute-done.3
  573.8 23.4 %while.114 = (s32[]{:T(128)}, f32[16,1,128]{2,0,1:T(8,128)S(1)}, f32[16,1,16,128]{3,2,1,0:T(8,128)S(1)}, f32[16,1,16,128]{3,0,2,1:T(8,128)S(1)}, f32[16,16,16,12...) while((s32[]{:T(128)}, f32[16,1,128]{2,0,1:T(8,128)S(1)}, ...), condition=%wide.region_7.8_spmd, body=%wide.region_6.7_spmd.sunk | while | flops 65542 | bytes 450711 | solution.py:85
  (3669 shorter events, 397.5 us)
Async XLA Ops:
  6.5 18.5 %copy-start.4 = (s32[1,128]{1,0:T(1,128)S(1)}, s32[1,128]{1,0:T(1,128)}, u32[]{:S(2)}) copy-start(s32[1,128]{1,0:T(1,128)} %param.86) | copy-start | bytes 1540
  6.5 95.9 %all-gather.3.cloned.1.call-start = ((), (), s32[]{:S(2)}) async-start(), calls=%async_computation | async-start | bytes 1056768 | tf_op jit(solution)/shard_map/all_gather | solution.py:108
  7.5 76.8 %collective-permute-start = (f32[16,16,1,128]{3,0,1,2:T(8,128)S(1)}, f32[16,16,1,128]{3,0,1,2:T(8,128)S(1)}, u32[]{:S(2)}, u32[]{:S(2)}) collective-permute-start(f32[16,16,1,128]{3,0,1,2:T(8,128)S(1)} %copy.131), channel_id=1, source_target_pairs={{0,1},{1,2},{2,3},{3,4},{4,5},{5,6},{6,7},{7,8},{8,9},{9,10},{10,1... | collective-permute-start | bytes 393224 | tf_op jit(solution)/shard_map/ppermute | solution.py:14
  9.4 74.9 %collective-permute-start.1 = (f32[16,16,1,128]{3,0,1,2:T(8,128)S(1)}, f32[16,16,1,128]{3,0,1,2:T(8,128)S(1)}, u32[]{:S(2)}, u32[]{:S(2)}) collective-permute-start(f32[16,16,1,128]{3,0,1,2:T(8,128)S(1)} %copy.131), channel_id=1, source_target_pairs={{1,0},{2,1},{3,2},{4,3},{5,4},{6,5},{7,6},{8,7},{9,8},{10,9},{11,1... | collective-permute-start | bytes 393224 | tf_op jit(solution)/shard_map/ppermute | solution.py:17
  57.4 4.3 copy-start.3
  57.4 19.4 %slice-start = ((s8[16777216]{0:T(1024)(128)(4,1)}), s8[4194304]{0:T(1024)(128)(4,1)S(1)}, s32[]{:S(2)}) async-start(s8[16777216]{0:T(1024)(128)(4,1)} %bitcast.631), calls=%async_computation.1 | async-start | bytes 8388608
  61.7 15.1 %slice-start.1 = ((s8[16777216]{0:T(1024)(128)(4,1)}), s8[4194304]{0:T(1024)(128)(4,1)S(1)}, s32[]{:S(2)}) async-start(s8[16777216]{0:T(1024)(128)(4,1)} %bitcast.631), calls=%async_computation.2 | async-start | bytes 8388608
  61.7 15.1 %slice-start.2 = ((s8[16777216]{0:T(1024)(128)(4,1)}), s8[4194304]{0:T(1024)(128)(4,1)S(1)}, s32[]{:S(2)}) async-start(s8[16777216]{0:T(1024)(128)(4,1)} %bitcast.631), calls=%async_computation.3 | async-start | bytes 8388608
  61.7 15.1 %slice-start.3 = ((s8[16777216]{0:T(1024)(128)(4,1)}), s8[4194304]{0:T(1024)(128)(4,1)S(1)}, s32[]{:S(2)}) async-start(s8[16777216]{0:T(1024)(128)(4,1)} %bitcast.631), calls=%async_computation.4 | async-start | bytes 8388608
  61.7 15.1 %copy-start.2 = (f32[16,128]{1,0:T(8,128)S(1)}, f32[16,128]{1,0:T(8,128)}, u32[]{:S(2)}) copy-start(f32[16,128]{1,0:T(8,128)} %get-tuple-element.1778) | copy-start | bytes 24580
  76.8 6.5 %copy-start.7 = (s32[1,128]{1,0:T(1,128)S(1)}, s32[1,128]{1,0:T(1,128)}, u32[]{:S(2)}) copy-start(s32[1,128]{1,0:T(1,128)} %param.87) | copy-start | bytes 1540
  76.9 7.4 %copy-start.6 = (s32[128]{0:T(128)S(1)}, s32[128]{0:T(128)}, u32[]{:S(2)}) copy-start(s32[128]{0:T(128)} %fusion.21) | copy-start | bytes 1540
  76.9 7.5 %copy-start = (f32[16,16,1,128]{3,2,1,0:T(1,128)S(1)}, f32[16,16,1,128]{3,2,1,0:T(1,128)}, u32[]{:S(2)}) copy-start(f32[16,16,1,128]{3,2,1,0:T(1,128)} %param.82) | copy-start | bytes 393220
  76.9 27.0 %copy-start.5 = (pred[128]{0:T(512)(128)(4,1)S(1)}, pred[128]{0:T(512)(128)(4,1)}, u32[]{:S(2)}) copy-start(pred[128]{0:T(512)(128)(4,1)} %compare_and_fusion) | copy-start | bytes 388
  290.3 4.9 collective-permute-start.2
  568.2 5.5 collective-permute-start.3
  597.2 0.7 copy-start.1
Sparse Core Ops, SparseCore 0:
  21.2 81.1 all-gather.2
where the time goes:
time: 611 us; the launch traced here: 605 us
  local copies, waits for them, and re-layouts  330 us (54%)
  other arithmetic  110 us (18%)
  matrix products  86.9 us (14%)
  waiting for transfers between devices  25.5 us (4%)
  loops' own time  23.4 us (4%)
  starting transfers between devices  15.1 us (2%)
  between operations  13.8 us (2%)
    dot_general x32, matrix products, product(): return jnp.einsum('vwc,wuc->vuc', left, right, precision=precise)  86.9 us
    dynamic_update_slice x48, local copies, waits for them, and re-layouts, advance(): blocks = lax.dynamic_update_index_in_dim(blocks, block_next, level, 2)  84.7 us
    while x48, other arithmetic  50.4 us
    scatter x512, local copies, waits for them, and re-layouts, solve_block(): augmented = augmented.at[pivot].set(pivot_row)  44.3 us
    dynamic_slice x32, local copies, waits for them, and re-layouts, retreat(): block = lax.dynamic_index_in_dim(blocks, level, 2, keepdims=False)  42.4 us
    slice x32, local copies, waits for them, and re-layouts, solve_block(): pivot_row = augmented[pivot] / augmented[pivot, pivot][None, :]  32.9 us
    squeeze x32, local copies, waits for them, and re-layouts, advance(): above = lax.dynamic_index_in_dim(upper, level, 2, keepdims=False)  29.3 us
    unnamed x28, local copies, waits for them, and re-layouts  24.4 us
  transfers between devices with their start and end apart: 5, of which 3 were waited for; matrix products, arithmetic and copies ran while one was open for 11% of the time, Pallas kernels for 0%

commit v1 on v0

v1 whole, which is shorter than its diff:
```python
import jax
import jax.numpy as jnp
from jax import lax
from jax.experimental import pallas as pl
from jax.experimental.pallas import tpu as pltpu
from jax.sharding import PartitionSpec as P


N = 16
T = 16
LANES = 128
F32 = jnp.float32


def spread(row, lane):
    return jnp.broadcast_to(row[lane:lane + 1, :], (8, LANES))


def repeat(ref, row):
    return ref[pl.ds(row, 8, stride=0), :]


def pair(ref, base):
    return ref[pl.ds(base, 8), :], ref[pl.ds(base + 8, 8), :]


def total(terms):
    terms = list(terms)
    while len(terms) > 1:
        terms = [a + b for a, b in zip(terms[::2], terms[1::2])] + terms[len(terms) & ~1:]
    return terms[0]


def coupled(lo, hi, w_ref, v_ref):
    lo, hi = list(lo), list(hi)
    v = [pair(v_ref, p * N) for p in range(N)]
    for r in range(N):
        m = [repeat(w_ref, p * N + r) for p in range(N)]
        if r < 8:
            lo[r] = lo[r] - total(m[p] * v[p][0] for p in range(N))
        hi[r] = hi[r] - total(m[p] * v[p][1] for p in range(N))
    return lo, hi


def forward(lo, hi, wlo, whi, u_put, i_put, w_ref, v_ref):
    lo, hi, wlo, whi = list(lo), list(hi), list(wlo), list(whi)
    for q in range(N // 2):
        p0, p1 = 2 * q, 2 * q + 1
        own = lo if p0 < 8 else hi
        s = p0 % 8
        r0, r1 = own[p0], own[p1]
        h0, h1 = hi[p0], hi[p1]
        a, b, c = spread(r0, s), spread(r0, s + 1), spread(r1, s + 1)
        r = 1.0 / (a * c - b * b)
        i00, i01, i11 = c * r, -(b * r), a * r
        i_put(q, (i00, i01, i11))

        def norm(x):
            return i00 * x[p0] + i01 * x[p1], i01 * x[p0] + i11 * x[p1]

        uhi = norm(hi)
        ulo = norm(lo) if p0 < 8 else None
        vlo, vhi = norm(wlo), norm(whi)
        for k, p in enumerate((p0, p1)):
            u_put(p, ulo[k] if p0 < 8 else None, uhi[k])
            w_ref[pl.ds(p * N, 8), :] = wlo[p]
            w_ref[pl.ds(p * N + 8, 8), :] = whi[p]
            v_ref[pl.ds(p * N, 8), :] = vlo[k]
            v_ref[pl.ds(p * N + 8, 8), :] = vhi[k]
        for v in range(p1 + 1, N):
            if v < 8:
                m0, m1 = spread(r0, v), spread(r1, v)
                lo[v] = lo[v] - (m0 * ulo[0] + m1 * ulo[1])
            else:
                m0, m1 = spread(h0, v - 8), spread(h1, v - 8)
            hi[v] = hi[v] - (m0 * uhi[0] + m1 * uhi[1])
            wlo[v] = wlo[v] - (m0 * vlo[0] + m1 * vlo[1])
            whi[v] = whi[v] - (m0 * vhi[0] + m1 * vhi[1])


def backward(u_ref, u_base, v_ref, g_ref, g_base):
    g = [list(pair(v_ref, p * N)) for p in range(N)]
    for q in reversed(range(N // 2)):
        for p in (2 * q, 2 * q + 1):
            for v in range(2 * q + 2, N):
                m = repeat(u_ref, u_base + p * N + v)
                g[p][0] = g[p][0] - m * g[v][0]
                g[p][1] = g[p][1] - m * g[v][1]
    for p in range(N):
        g_ref[pl.ds(g_base + p * N, 8), :] = g[p][0]
        g_ref[pl.ds(g_base + p * N + 8, 8), :] = g[p][1]


def going_up():
    return lax.axis_index("wall") == 0


def factor_kernel(
    jac, length_ref, g_ref, u_ref, i_ref, s_ref, p_ref, m_buf, c_buf, w_a, v_a, w_b, v_b, m_sem, c_sem
):
    up = going_up()
    side = jnp.where(up, 2, 0)

    def copies(t):
        lev = jnp.where(up, t, T - 1 - t)
        return (
            pltpu.make_async_copy(jac.at[1, :, :, lev, 0, :], m_buf.at[t], m_sem.at[t]),
            pltpu.make_async_copy(jac.at[side, :, :, lev, 0, :], c_buf.at[t], c_sem.at[t]),
        )

    for t in range(T):
        for copy in copies(t):
            copy.start()
    length = jnp.broadcast_to(length_ref[...], (8, LANES))
    sub = lax.broadcasted_iota(jnp.int32, (8, LANES), 0)
    zero = jnp.zeros((8, LANES), F32)
    w_b[...] = jnp.zeros(w_b.shape, F32)
    v_b[...] = jnp.zeros(v_b.shape, F32)

    def level(t, w_p, v_p, w_t, v_t):
        for copy in copies(t):
            copy.wait()
        active = jnp.where(up, 0, 2 * T - 1 - t) < length
        linked = jnp.where(up, t + 1, 2 * T - 1 - t) < length
        lo, hi, wlo, whi = [], [], [], []
        for r in range(N):
            eye = jnp.where(sub == r % 8, 1.0, 0.0)
            if r < 8:
                lo.append(jnp.where(active, m_buf[t, r, 0:8, :], eye))
            hi.append(jnp.where(active, m_buf[t, r, 8:16, :], zero if r < 8 else eye))
            wlo.append(jnp.where(linked, c_buf[t, r, 0:8, :], 0.0))
            whi.append(jnp.where(linked, c_buf[t, r, 8:16, :], 0.0))
        lo, hi = coupled(lo, hi, w_p, v_p)
        for r in range(N):
            if r < 8:
                s_ref[pl.ds(r * N, 8), :] = lo[r]
            s_ref[pl.ds(r * N + 8, 8), :] = hi[r]

        def u_put(p, low, high):
            if low is not None:
                u_ref[pl.ds(t * 256 + p * N, 8), :] = low
            u_ref[pl.ds(t * 256 + p * N + 8, 8), :] = high

        def i_put(q, values):
            for k, value in enumerate(values):
                i_ref[pl.ds(t * 24 + q * 3 + k, 1), :] = value[0:1, :]

        forward(lo, hi, wlo, whi, u_put, i_put, w_t, v_t)
        backward(u_ref, t * 256, v_t, g_ref, t * 256)

    def body(h, carry):
        level(2 * h, w_b, v_b, w_a, v_a)
        level(2 * h + 1, w_a, v_a, w_b, v_b)
        return carry

    lax.fori_loop(0, T // 2, body, 0)
    lo, hi = coupled([zero] * 8, [zero] * N, w_b, v_b)
    for r in range(N):
        p_ref[pl.ds(r * N, 8), :] = lo[r] if r < 8 else zero
        p_ref[pl.ds(r * N + 8, 8), :] = hi[r]


def source_kernel(
    jac, residual, here, before, after, coupling, face, partner_ref, length_ref, flag_ref, g_ref,
    y_ref, q_ref, s_buf, k_buf, k_sem
):
    up = going_up()
    copy = pltpu.make_async_copy(jac.at[0, :, :, 0, 0, :], k_buf, k_sem)
    copy.start()
    length = jnp.broadcast_to(length_ref[...], (8, LANES))
    sub = lax.broadcasted_iota(jnp.int32, (8, LANES), 0)
    active = [jnp.where(up, 0, T) + 8 * h + sub < length for h in range(2)]
    for r in range(N):
        for h in range(2):
            at = pl.ds(r * T + 8 * h, 8)
            c = [coupling[pl.ds(m * N * T + r * T + 8 * h, 8), :] for m in range(4)]
            own = here[at, :]
            value = residual[at, :] + (
                (c[0] * before[at, :] + c[1] * after[at, :])
                + (c[2] * pltpu.roll(own, 1, 1) + c[3] * pltpu.roll(own, LANES - 1, 1))
            )
            s_buf[at, :] = jnp.where(active[h], value, 0.0)

    index = jnp.broadcast_to(partner_ref[...], (8, LANES))
    facing = [jnp.take_along_axis(face[pl.ds(8 * h, 8), :], index, axis=1) for h in range(2)]
    copy.wait()
    rows = k_buf.reshape(N * N, LANES)
    weight = jnp.broadcast_to(flag_ref[...].astype(F32), (8, LANES)) * jnp.where(up, 1.0, 0.0)

    def at_level(t):
        lev = jnp.where(up, t, T - 1 - t)
        return [s_buf[pl.ds(lev + 8 * h * T, 8, stride=T), :] for h in range(2)]

    m = [spread(facing[w // 8], w % 8) for w in range(N)]
    y = at_level(0)
    for h in range(2):
        wake = total(rows[pl.ds(h * 8 * N + w, 8, stride=N), :] * m[w] for w in range(N))
        y[h] = y[h] - weight * wake
    for t in range(T):
        for h in range(2):
            y_ref[pl.ds(8 * h * T + t, 8, stride=T), :] = y[h]
        m = [spread(y[p // 8], p % 8) for p in range(N)]
        sums = [total(g_ref[pl.ds(t * 256 + p * N + 8 * h, 8), :] * m[p] for p in range(N)) for h in range(2)]
        if t + 1 < T:
            y = [a - b for a, b in zip(at_level(t + 1), sums)]
        else:
            for h in range(2):
                q_ref[pl.ds(8 * h, 8), :] = sums[h]


def inner_kernel(u_ref, i_ref, y_ref, s_ref, p_ref, x_ref, inv_ref, w_buf, v_buf, u_buf):
    for h in range(2):
        def u(p, v):
            return u_ref[pl.ds(h * 8 * 256 + p * N + v, 8, stride=256), :]

        def i(q, k):
            return i_ref[pl.ds(h * 8 * 24 + q * 3 + k, 8, stride=24), :]

        y = [y_ref[pl.ds(p * T + 8 * h, 8), :] for p in range(N)]
        z = [None] * N
        for q in range(N // 2):
            p0, p1 = 2 * q, 2 * q + 1
            for v in range(p1 + 1, N):
                y[v] = y[v] - (u(p0, v) * y[p0] + u(p1, v) * y[p1])
            i00, i01, i11 = i(q, 0), i(q, 1), i(q, 2)
            z[p0] = i00 * y[p0] + i01 * y[p1]
            z[p1] = i01 * y[p0] + i11 * y[p1]
        for q in reversed(range(N // 2)):
            for p in (2 * q, 2 * q + 1):
                for v in range(2 * q + 2, N):
                    z[p] = z[p] - u(p, v) * z[v]
        for p in range(N):
            x_ref[pl.ds(p * T + 8 * h, 8), :] = z[p]

    sub = lax.broadcasted_iota(jnp.int32, (8, LANES), 0)
    zero = jnp.zeros((8, LANES), F32)
    lo = [s_ref[pl.ds(r * N, 8), :] + p_ref[pl.ds(r * N, 8), :] for r in range(8)]
    hi = [s_ref[pl.ds(r * N + 8, 8), :] + p_ref[pl.ds(r * N + 8, 8), :] for r in range(N)]
    eye = [jnp.where(sub == r, 1.0, 0.0) for r in range(8)]

    def u_put(p, low, high):
        if low is not None:
            u_buf[pl.ds(p * N, 8), :] = low
        u_buf[pl.ds(p * N + 8, 8), :] = high

    forward(lo, hi, eye + [zero] * 8, [zero] * 8 + eye, u_put, lambda q, v: None, w_buf, v_buf)
    backward(u_buf, 0, v_buf, inv_ref, 0)


def outer_kernel(g_ref, x0_ref, inv_ref, y_ref, q_ref, x_ref):
    up = going_up()
    last = T - 1
    rhs = [y_ref[pl.ds(8 * h * T + last, 8, stride=T), :] - q_ref[pl.ds(8 * h, 8), :] for h in range(2)]
    m = [spread(rhs[p // 8], p % 8) for p in range(N)]
    x = [total(inv_ref[pl.ds(p * N + 8 * h, 8), :] * m[p] for p in range(N)) for h in range(2)]
    for t in reversed(range(T)):
        if t < last:
            m = [spread(x[v // 8], v % 8) for v in range(N)]
            x = [
                x0_ref[pl.ds(8 * h * T + t, 8, stride=T), :]
                - total(g_ref[pl.ds(t * 256 + 8 * h * N + v, 8, stride=N), :] * m[v] for v in range(N))
                for h in range(2)
            ]
        lev = jnp.where(up, t, last - t)
        for h in range(2):
            x_ref[pl.ds(lev + 8 * h * T, 8, stride=T), :] = x[h]


def shape(rows):
    return jax.ShapeDtypeStruct((rows, LANES), F32)


ANY = pl.BlockSpec(memory_space=pl.ANY)
LOCAL = pl.BlockSpec(memory_space=pltpu.VMEM)


def call(kernel, name, outs, ins, scratch, args, flops):
    return pl.pallas_call(
        kernel,
        out_shape=tuple(shape(rows) for rows in outs),
        in_specs=ins,
        out_specs=[LOCAL] * len(outs),
        scratch_shapes=scratch,
        compiler_params=pltpu.CompilerParams(vmem_limit_bytes=24 * 2**20),
        cost_estimate=pl.CostEstimate(flops=flops, bytes_accessed=4 * 2**20, transcendentals=0),
        name=name,
    )(*args)


def per_device(
    jacobian, residual, previous_update, offline_coupling, wake_partner, line_length, bottom_flag
):
    planes = lax.axis_size("plane")
    block = pltpu.VMEM((N * N, LANES), F32)
    here = previous_update.reshape(N * T, LANES)
    forth = [(i, i + 1) for i in range(planes - 1)]
    before = lax.ppermute(here, "plane", forth)
    after = lax.ppermute(here, "plane", [(b, a) for a, b in forth])
    face = lax.ppermute(
        previous_update[:, 0, 0], "plane", [(i, (i + planes // 2) % planes) for i in range(planes)]
    )
    g, u, i, s, p = call(
        factor_kernel,
        "factor",
        (T * 256, T * 256, T * 24, 256, 256),
        [ANY, LOCAL],
        [pltpu.VMEM((T, N, N, LANES), F32)] * 2
        + [block] * 4
        + [pltpu.SemaphoreType.DMA((T,))] * 2,
        (jacobian, line_length),
        T * 128 * 2 * 12000,
    )
    swap = [(0, 1), (1, 0)]
    p = lax.ppermute(p, "wall", swap)
    y, q = call(
        source_kernel,
        "source",
        (256, 16),
        [ANY] + [LOCAL] * 10,
        [block, pltpu.VMEM((N, N, LANES), F32), pltpu.SemaphoreType.DMA],
        (
            jacobian,
            residual.reshape(N * T, LANES),
            here,
            before,
            after,
            offline_coupling.reshape(4 * N * T, LANES),
            face,
            wake_partner,
            line_length,
            bottom_flag,
            g,
        ),
        T * 128 * 2 * 800,
    )
    q = lax.ppermute(q, "wall", swap)
    x, inverse = call(
        inner_kernel, "inner", (256, 256), [LOCAL] * 5, [block] * 3, (u, i, y, s, p), T * 128 * 2 * 1000
    )
    (update,) = call(
        outer_kernel, "outer", (256,), [LOCAL] * 5, [], (g, x, inverse, y, q), T * 128 * 2 * 300
    )
    return update.reshape(N, T, 1, LANES)


def solution(mesh):
    return jax.shard_map(
        per_device,
        mesh=mesh,
        in_specs=(
            P(None, None, None, "wall", "plane", None),
            P(None, "wall", "plane", None),
            P(None, "wall", "plane", None),
            P(None, None, "wall", "plane", None),
            P("plane", None),
            P("plane", None),
            P("plane", None),
        ),
        out_specs=P(None, "wall", "plane", None),
        check_vma=False,
    )
```

time: 611 us -> 37.7 us (0.06); the launches traced: 605 us -> 37.5 us
  local copies, waits for them, and re-layouts: 330 us -> 3.46 us
  other arithmetic: 110 us -> 0 us
  matrix products: 86.9 us -> 0 us
  loops' own time: 23.4 us -> 0 us
  waiting for transfers between devices: 25.5 us -> 5.79 us
  between operations: 13.8 us -> 0.09 us
  Pallas kernels: 0 us -> 12.4 us
    dot_general x32 -> x0, matrix products: 86.9 us -> none  [product(): return jnp.einsum('vwc,wuc->vuc', left, right, precision=precise)]
    dynamic_update_slice x112 -> x0, local copies, waits for them, and re-layouts: 86.5 us -> none  [the longest x48 84.7 us: advance(): blocks = lax.dynamic_update_index_in_dim(blocks, block_next, level, 2)]
    slice x89 -> x1, local copies, waits for them, and re-layouts: 59.1 us -> 0.01 us  [per_device(): previous_update[:, 0, 0]]
    while x48 -> x0, other arithmetic: 50.4 us -> none
    scatter x512 -> x0, local copies, waits for them, and re-layouts: 44.3 us -> none  [solve_block(): augmented = augmented.at[pivot].set(pivot_row)]
    dynamic_slice x34 -> x0, local copies, waits for them, and re-layouts: 43.2 us -> none  [the longest x32 42.4 us: retreat(): block = lax.dynamic_index_in_dim(blocks, level, 2, keepdims=False)]
    squeeze x34 -> x0, local copies, waits for them, and re-layouts: 30.2 us -> none  [the longest x32 29.3 us: advance(): above = lax.dynamic_index_in_dim(upper, level, 2, keepdims=False)]
    another operation x4 -> x0, loops' own time: 23.4 us -> none  [the longest x2 21.7 us: eliminate(): lax.fori_loop(0, levels, advance, (block_in, vector_in, blocks, vectors))]
  transfers between devices with their start and end apart: 5 -> 5, of which waited for: 3 -> 2; matrix products, arithmetic and copies ran while one was open for 11% -> 0% of each run, Pallas kernels for 0% -> 29%
where the time goes in v1:
time: 37.7 us; the launch traced here: 37.5 us
  starting transfers between devices  15.8 us (42%)
  Pallas kernels  12.4 us (33%)
  waiting for transfers between devices  5.79 us (15%)
  local copies, waits for them, and re-layouts  3.46 us (9%)
    pallas_call x4, Pallas kernels, call(): pl.pallas_call(kernel, out_shape=tuple((shape(rows) for rows in outs)), i...  12.4 us
    ppermute x1, starting transfers between devices, per_device(): after = lax.ppermute(here, 'plane', [(b, a) for a, b in forth])  10.5 us
    ppermute x1, waiting for transfers between devices, per_device(): lax.ppermute(previous_update[:, 0, 0], 'plane', [(i, (i + planes // 2) %...  4.04 us
    unnamed x14, local copies, waits for them, and re-layouts  3.45 us
    ppermute x1, starting transfers between devices, per_device(): before = lax.ppermute(here, 'plane', forth)  1.92 us
    ppermute x1, waiting for transfers between devices, per_device(): q = lax.ppermute(q, 'wall', swap)  1.74 us
    ppermute x1, starting transfers between devices, per_device(): lax.ppermute(previous_update[:, 0, 0], 'plane', [(i, (i + planes // 2) %...  1.2 us
    ppermute x1, starting transfers between devices, per_device(): p = lax.ppermute(p, 'wall', swap)  1.11 us
  transfers between devices with their start and end apart: 5, of which 2 were waited for; matrix products, arithmetic and copies ran while one was open for 0% of the time, Pallas kernels for 29%

profile of v1, /device:TPU:6, one launch (start us, length us, event | category | flops | bytes accessed | tf_op | source)
XLA Modules:
  0.0 37.5 jit_solution(254898157799108719)
XLA Ops:
  0.0 0.0 copy-start.5
  0.0 0.0 copy-start.6
  0.0 10.5 %collective-permute-start.1 = (f32[256,128]{1,0:T(8,128)}, f32[256,128]{1,0:T(8,128)S(1)}, u32[]{:S(2)}, u32[]{:S(2)}) collective-permute-start(f32[256,128]{1,0:T(8,128)} %bitcast.10), channel_id=1, source_target_pairs={{1,0},{2,1},{3,2},{4,3},{5,4},{6,5},{7,6},{8,7},{9,8},{10,9},{11,1... | collective-permute-start | bytes 393224 | tf_op jit(solution)/shard_map/ppermute | solution.py:298
  10.5 1.9 %collective-permute-start = (f32[256,128]{1,0:T(8,128)}, f32[256,128]{1,0:T(8,128)S(1)}, u32[]{:S(2)}, u32[]{:S(2)}) collective-permute-start(f32[256,128]{1,0:T(8,128)} %bitcast.11), channel_id=1, source_target_pairs={{0,1},{1,2},{2,3},{3,4},{4,5},{5,6},{6,7},{7,8},{8,9},{9,10},{10,1... | collective-permute-start | bytes 393224 | tf_op jit(solution)/shard_map/ppermute | solution.py:297
  12.4 0.0 copy-start
  12.4 2.8 %copy-done = f32[3,16,16,16,1,128]{5,4,3,2,1,0:T(1,128)S(1)} copy-done((f32[3,16,16,16,1,128]{5,4,3,2,1,0:T(1,128)S(1)}, f32[3,16,16,16,1,128]{5,4,3,2,1,0:T(1,128)}, u32[]{:S(2)}) %copy-start) | copy-done | bytes 6291480
  15.2 0.0 copy-start.4
  15.2 0.7 %copy-done.4 = s32[1,128]{1,0:T(1,128)S(1)} copy-done((s32[1,128]{1,0:T(1,128)S(1)}, s32[1,128]{1,0:T(1,128)}, u32[]{:S(2)}) %copy-start.4) | copy-done | bytes 536
  15.9 0.0 copy-start.2
  15.9 0.0 copy-start.1
  15.9 0.0 copy-start.3
  15.9 9.6 %factor.1 = (f32[4096,128]{1,0:T(8,128)S(1)}, f32[4096,128]{1,0:T(8,128)S(1)}, f32[384,128]{1,0:T(8,128)S(1)}, f32[256,128]{1,0:T(8,128)S(1)}, f32[256,128]{1,0:T(8,128)S(1)}) custom-call(f32[3,16,16,16,1,128]{5,4,3,2,1,0:T(1,128)S(1)} %copy-done, s32[1,128]{1,0:T(1,128)S(1)} %copy-done.4), custom_call_target="tpu_custom_call" | custom-call | flops 49152000 | bytes 4194304 | tf_op jit(solution)/shard_map/factor/pallas_call | solution.py:278
  25.5 1.1 %collective-permute-start.3 = (f32[256,128]{1,0:T(8,128)S(1)}, f32[256,128]{1,0:T(8,128)S(1)}, u32[]{:S(2)}, u32[]{:S(2)}) collective-permute-start(f32[256,128]{1,0:T(8,128)S(1)} %get-tuple-element.19), channel_id=1, source_target_pairs={{0,128},{128,0},{1,129},{129,1},{2,130},{130,2},{3,131},{131,3},{4... | collective-permute-start | bytes 393224 | tf_op jit(solution)/shard_map/ppermute | solution.py:314
  26.6 0.0 copy-done.2
  26.6 1.2 %collective-permute-start.2 = (f32[16,128]{1,0:T(8,128)S(1)}, f32[16,128]{1,0:T(8,128)S(1)}, u32[]{:S(2)}, u32[]{:S(2)}) collective-permute-start(f32[16,128]{1,0:T(8,128)S(1)} %bitcast.14), channel_id=1, source_target_pairs={{0,64},{1,65},{2,66},{3,67},{4,68},{5,69},{6,70},{7,71},{8,72},{9,... | collective-permute-start | bytes 24584 | tf_op jit(solution)/shard_map/ppermute | solution.py:299
  27.8 4.0 %collective-permute-done.2.face = f32[16,128]{1,0:T(8,128)S(1)} collective-permute-done((f32[16,128]{1,0:T(8,128)S(1)}, f32[16,128]{1,0:T(8,128)S(1)}, u32[]{:S(2)}, u32[]{:S(2)}) %collective-permute-start.2) | collective-permute-done | bytes 8224 | tf_op jit(solution)/shard_map/ppermute | solution.py:299
  31.9 0.0 collective-permute-done.1.after
  31.9 0.0 collective-permute-done.before
  31.9 0.0 copy-done.5
  31.9 0.0 copy-done.6
  31.9 0.0 copy-done.1
  31.9 0.0 copy-done.3
  31.9 0.5 %source.1 = (f32[256,128]{1,0:T(8,128)S(1)}, f32[16,128]{1,0:T(8,128)S(1)}) custom-call(f32[3,16,16,16,1,128]{5,4,3,2,1,0:T(1,128)S(1)} %copy-done, f32[256,128]{1,0:T(8,128)S(1)} %bitcast.13, f32[256,128]{1,0:T(8,128)S(1)} %bitcast.12, f32[256,128]{1,0:T(8,128)S(1)} %collective-permute-done.before, f32[256,128]{1,0:T(8,128)S(1)} %collective-permute-done.1.after, ...), custom_call_target="tpu_custom_call" | custom-call | flops 3276800 | bytes 4194304 | tf_op jit(solution)/shard_map/source/pallas_call | solution.py:278
  32.5 1.1 %collective-permute-start.4 = (f32[16,128]{1,0:T(8,128)S(1)}, f32[16,128]{1,0:T(8,128)S(1)}, u32[]{:S(2)}, u32[]{:S(2)}) collective-permute-start(f32[16,128]{1,0:T(8,128)S(1)} %get-tuple-element.22), channel_id=1, source_target_pairs={{0,128},{128,0},{1,129},{129,1},{2,130},{130,2},{3,131},{131,3},{4... | collective-permute-start | bytes 24584 | tf_op jit(solution)/shard_map/ppermute | solution.py:336
  33.6 0.0 collective-permute-done.3.p_ref
  33.6 0.9 %inner.1 = (f32[256,128]{1,0:T(8,128)S(1)}, f32[256,128]{1,0:T(8,128)S(1)}) custom-call(f32[4096,128]{1,0:T(8,128)S(1)} %get-tuple-element.15.u_ref, f32[384,128]{1,0:T(8,128)S(1)} %get-tuple-element.16.i_ref, f32[256,128]{1,0:T(8,128)S(1)} %get-tuple-element.17.y_ref, f32[256,128]{1,0:T(8,128)S(1)} %get-tuple-element.18.s_ref, ...), custom_call_target="tpu_custom_call" | custom-call | flops 4096000 | bytes 4194304 | tf_op jit(solution)/shard_map/inner/pallas_call | solution.py:278
  34.5 1.7 %collective-permute-done.4.q_ref = f32[16,128]{1,0:T(8,128)S(1)} collective-permute-done((f32[16,128]{1,0:T(8,128)S(1)}, f32[16,128]{1,0:T(8,128)S(1)}, u32[]{:S(2)}, u32[]{:S(2)}) %collective-permute-start.4) | collective-permute-done | bytes 8224 | tf_op jit(solution)/shard_map/ppermute | solution.py:336
  36.2 1.3 %outer.1 = f32[256,128]{1,0:T(8,128)} custom-call(f32[4096,128]{1,0:T(8,128)S(1)} %get-tuple-element.14.g_ref, f32[256,128]{1,0:T(8,128)S(1)} %get-tuple-element.20.x0_ref, f32[256,128]{1,0:T(8,128)S(1)} %get-tuple-element.21.inv_ref, f32[256,128]{1,0:T(8,128)S(1)} %get-tuple-element.17.y_ref, f32[16,128]{1,0:T(8,128)S(1)} %collective-permute-done.4.q_ref), custom_call_target="tpu_custom_call" | custom-call | flops 1228800 | bytes 4194304 | tf_op jit(solution)/shard_map/outer/pallas_call | solution.py:278
  (1 shorter events, 0.0 us)
Async XLA Ops:
  0.0 31.9 %copy-start.5 = (s32[1,128]{1,0:T(1,128)S(1)}, s32[1,128]{1,0:T(1,128)}, u32[]{:S(2)}) copy-start(s32[1,128]{1,0:T(1,128)} %partner_ref.1) | copy-start | bytes 1540
  0.0 31.9 %copy-start.6 = (s32[1,128]{1,0:T(1,128)S(1)}, s32[1,128]{1,0:T(1,128)}, u32[]{:S(2)}) copy-start(s32[1,128]{1,0:T(1,128)} %flag_ref.1) | copy-start | bytes 1540
  0.0 31.9 %collective-permute-start.1 = (f32[256,128]{1,0:T(8,128)}, f32[256,128]{1,0:T(8,128)S(1)}, u32[]{:S(2)}, u32[]{:S(2)}) collective-permute-start(f32[256,128]{1,0:T(8,128)} %bitcast.10), channel_id=1, source_target_pairs={{1,0},{2,1},{3,2},{4,3},{5,4},{6,5},{7,6},{8,7},{9,8},{10,9},{11,1... | collective-permute-start | bytes 393224 | tf_op jit(solution)/shard_map/ppermute | solution.py:298
  10.5 21.4 %collective-permute-start = (f32[256,128]{1,0:T(8,128)}, f32[256,128]{1,0:T(8,128)S(1)}, u32[]{:S(2)}, u32[]{:S(2)}) collective-permute-start(f32[256,128]{1,0:T(8,128)} %bitcast.11), channel_id=1, source_target_pairs={{0,1},{1,2},{2,3},{3,4},{4,5},{5,6},{6,7},{7,8},{8,9},{9,10},{10,1... | collective-permute-start | bytes 393224 | tf_op jit(solution)/shard_map/ppermute | solution.py:297
  12.4 2.8 %copy-start = (f32[3,16,16,16,1,128]{5,4,3,2,1,0:T(1,128)S(1)}, f32[3,16,16,16,1,128]{5,4,3,2,1,0:T(1,128)}, u32[]{:S(2)}) copy-start(f32[3,16,16,16,1,128]{5,4,3,2,1,0:T(1,128)} %jac.3) | copy-start | bytes 18874372
  15.2 0.7 %copy-start.4 = (s32[1,128]{1,0:T(1,128)S(1)}, s32[1,128]{1,0:T(1,128)}, u32[]{:S(2)}) copy-start(s32[1,128]{1,0:T(1,128)} %length_ref.3) | copy-start | bytes 1540
  15.9 10.8 %copy-start.2 = (f32[16,16,1,128]{3,2,1,0:T(1,128)S(1)}, f32[16,16,1,128]{3,2,1,0:T(1,128)}, u32[]{:S(2)}) copy-start(f32[16,16,1,128]{3,2,1,0:T(1,128)} %param.9) | copy-start | bytes 393220
  15.9 16.0 %copy-start.1 = (f32[4,16,16,1,128]{4,3,2,1,0:T(1,128)S(1)}, f32[4,16,16,1,128]{4,3,2,1,0:T(1,128)}, u32[]{:S(2)}) copy-start(f32[4,16,16,1,128]{4,3,2,1,0:T(1,128)} %param.10) | copy-start | bytes 1572868
  15.9 16.0 %copy-start.3 = (f32[16,16,1,128]{3,2,1,0:T(1,128)S(1)}, f32[16,16,1,128]{3,2,1,0:T(1,128)}, u32[]{:S(2)}) copy-start(f32[16,16,1,128]{3,2,1,0:T(1,128)} %param.8) | copy-start | bytes 393220
  25.5 8.0 %collective-permute-start.3 = (f32[256,128]{1,0:T(8,128)S(1)}, f32[256,128]{1,0:T(8,128)S(1)}, u32[]{:S(2)}, u32[]{:S(2)}) collective-permute-start(f32[256,128]{1,0:T(8,128)S(1)} %get-tuple-element.19), channel_id=1, source_target_pairs={{0,128},{128,0},{1,129},{129,1},{2,130},{130,2},{3,131},{131,3},{4... | collective-permute-start | bytes 393224 | tf_op jit(solution)/shard_map/ppermute | solution.py:314
  26.6 5.2 %collective-permute-start.2 = (f32[16,128]{1,0:T(8,128)S(1)}, f32[16,128]{1,0:T(8,128)S(1)}, u32[]{:S(2)}, u32[]{:S(2)}) collective-permute-start(f32[16,128]{1,0:T(8,128)S(1)} %bitcast.14), channel_id=1, source_target_pairs={{0,64},{1,65},{2,66},{3,67},{4,68},{5,69},{6,70},{7,71},{8,72},{9,... | collective-permute-start | bytes 24584 | tf_op jit(solution)/shard_map/ppermute | solution.py:299
  32.5 3.7 %collective-permute-start.4 = (f32[16,128]{1,0:T(8,128)S(1)}, f32[16,128]{1,0:T(8,128)S(1)}, u32[]{:S(2)}, u32[]{:S(2)}) collective-permute-start(f32[16,128]{1,0:T(8,128)S(1)} %get-tuple-element.22), channel_id=1, source_target_pairs={{0,128},{128,0},{1,129},{129,1},{2,130},{130,2},{3,131},{131,3},{4... | collective-permute-start | bytes 24584 | tf_op jit(solution)/shard_map/ppermute | solution.py:336

commit v2 on v1

v2 whole, which is shorter than its diff:
```python
import jax
import jax.numpy as jnp
from jax import lax
from jax.experimental import pallas as pl
from jax.experimental.pallas import tpu as pltpu
from jax.sharding import PartitionSpec as P


N = 16
T = 16
LANES = 128
F32 = jnp.float32


def spread(row, lane):
    return jnp.broadcast_to(row[lane:lane + 1, :], (8, LANES))


def repeat(ref, row):
    return ref[pl.ds(row, 8, stride=0), :]


def pair(ref, base):
    return ref[pl.ds(base, 8), :], ref[pl.ds(base + 8, 8), :]


def total(terms):
    terms = list(terms)
    while len(terms) > 1:
        terms = [a + b for a, b in zip(terms[::2], terms[1::2])] + terms[len(terms) & ~1:]
    return terms[0]


def coupled(lo, hi, w_ref, v_ref, linked):
    lo, hi = list(lo), list(hi)
    v = [pair(v_ref, p * N) for p in range(N)]
    for r in range(N):
        m = [repeat(w_ref, p * N + r) for p in range(N)]
        if r < 8:
            lo[r] = lo[r] - jnp.where(linked, total(m[p] * v[p][0] for p in range(N)), 0.0)
        hi[r] = hi[r] - jnp.where(linked, total(m[p] * v[p][1] for p in range(N)), 0.0)
    return lo, hi


def forward(lo, hi, wlo, whi, u_put, i_put, w_ref, v_ref, b_ref):
    lo, hi, wlo, whi = list(lo), list(hi), list(wlo), list(whi)
    for q in range(N // 2):
        p0, p1, p2 = 2 * q, 2 * q + 1, 2 * q + 2
        own = lo if p0 < 8 else hi
        s = p0 % 8
        a, b, c = spread(own[p0], s), spread(own[p0], s + 1), spread(own[p1], s + 1)
        for p in (p0, p1):
            if p0 < 8:
                b_ref[pl.ds(p * N, 8), :] = lo[p]
            b_ref[pl.ds(p * N + 8, 8), :] = hi[p]
        r = 1.0 / (a * c - b * b)
        i00, i01, i11 = c * r, -(b * r), a * r
        i_put(q, (i00, i01, i11))

        def norm(x):
            return i00 * x[p0] + i01 * x[p1], i01 * x[p0] + i11 * x[p1]

        uhi = norm(hi)
        ulo = norm(lo) if p0 < 8 else None
        vlo, vhi = norm(wlo), norm(whi)
        for k, p in enumerate((p0, p1)):
            u_put(p, ulo[k] if p0 < 8 else None, uhi[k])
            w_ref[pl.ds(p * N, 8), :] = wlo[p]
            w_ref[pl.ds(p * N + 8, 8), :] = whi[p]
            v_ref[pl.ds(p * N, 8), :] = vlo[k]
            v_ref[pl.ds(p * N + 8, 8), :] = vhi[k]
        for v in range(p2, N):
            m0, m1 = repeat(b_ref, p0 * N + v), repeat(b_ref, p1 * N + v)
            if v < 8:
                lo[v] = lo[v] - (m0 * ulo[0] + m1 * ulo[1])
            hi[v] = hi[v] - (m0 * uhi[0] + m1 * uhi[1])
            wlo[v] = wlo[v] - (m0 * vlo[0] + m1 * vlo[1])
            whi[v] = whi[v] - (m0 * vhi[0] + m1 * vhi[1])


def backward(u_ref, u_base, v_ref, g_ref, g_base):
    g = [list(pair(v_ref, p * N)) for p in range(N)]
    for q in reversed(range(N // 2)):
        for p in (2 * q, 2 * q + 1):
            for v in range(2 * q + 2, N):
                m = repeat(u_ref, u_base + p * N + v)
                g[p][0] = g[p][0] - m * g[v][0]
                g[p][1] = g[p][1] - m * g[v][1]
    for p in range(N):
        g_ref[pl.ds(g_base + p * N, 8), :] = g[p][0]
        g_ref[pl.ds(g_base + p * N + 8, 8), :] = g[p][1]


def going_up():
    return lax.axis_index("wall") == 0


AHEAD = 4


def factor_kernel(
    jac, length_hbm,
    g_ref, u_ref, i_ref, s_ref, p_ref, k_ref,
    m_buf, c_buf, w_a, v_a, w_b, v_b, b_ref, l_buf, m_sem, c_sem, k_sem, l_sem
):
    up = going_up()
    side = jnp.where(up, 2, 0)

    def copies(t):
        lev = jnp.where(up, t, T - 1 - t)
        return (
            pltpu.make_async_copy(jac.at[1, :, :, lev, 0, :], m_buf.at[t], m_sem.at[t]),
            pltpu.make_async_copy(jac.at[side, :, :, lev, 0, :], c_buf.at[t], c_sem.at[t]),
        )

    def fetch(t):
        for copy in copies(t):
            copy.start()

    length_copy = pltpu.make_async_copy(length_hbm, l_buf, l_sem)
    length_copy.start()
    for t in range(AHEAD):
        fetch(t)
    wake_copy = pltpu.make_async_copy(jac.at[0, :, :, 0, 0, :], k_ref, k_sem)
    zero = jnp.zeros((8, LANES), F32)
    w_b[...] = jnp.zeros(w_b.shape, F32)
    v_b[...] = jnp.zeros(v_b.shape, F32)
    length_copy.wait()

    def linked(t):
        return jnp.where(up, t + 1, 2 * T - 1 - t) < jnp.broadcast_to(l_buf[...], (8, LANES))

    def level(t, w_p, v_p, w_t, v_t):
        for copy in copies(t):
            copy.wait()
        lo, hi, wlo, whi = [], [], [], []
        for r in range(N):
            lo.append(m_buf[t, r, 0:8, :])
            hi.append(m_buf[t, r, 8:16, :])
            wlo.append(c_buf[t, r, 0:8, :])
            whi.append(c_buf[t, r, 8:16, :])
        lo, hi = coupled(lo[:8], hi, w_p, v_p, linked(t - 1))
        for r in range(N):
            if r < 8:
                s_ref[pl.ds(r * 8, 8), :] = lo[r]
            s_ref[pl.ds(64 + r * 8, 8), :] = hi[r]

        def u_put(p, low, high):
            if low is not None:
                u_ref[pl.ds(t * 256 + p * N, 8), :] = low
            u_ref[pl.ds(t * 256 + p * N + 8, 8), :] = high

        def i_put(q, values):
            for k, value in enumerate(values):
                i_ref[pl.ds(t * 24 + q * 3 + k, 1), :] = value[0:1, :]

        forward(lo, hi, wlo, whi, u_put, i_put, w_t, v_t, b_ref)
        backward(u_ref, t * 256, v_t, g_ref, t * 256)

    def body(h, carry):
        @pl.when(h < (T - AHEAD) // 2)
        def _():
            fetch(2 * h + AHEAD)
            fetch(2 * h + AHEAD + 1)

        @pl.when(h == (T - AHEAD) // 2)
        def _():
            wake_copy.start()

        level(2 * h, w_b, v_b, w_a, v_a)
        level(2 * h + 1, w_a, v_a, w_b, v_b)
        return carry

    lax.fori_loop(0, T // 2, body, 0)
    lo, hi = coupled([zero] * 8, [zero] * N, w_b, v_b, linked(T - 1))
    for r, row in enumerate(lo + hi):
        p_ref[pl.ds(r * 8, 8), :] = row
    wake_copy.wait()


def source_kernel(
    k_buf, residual, here, face, near, far, coupling, partner_ref, length_ref, flag_ref, g_ref,
    y_ref, q_ref, s_buf
):
    up = going_up()
    length = jnp.broadcast_to(length_ref[...], (8, LANES))
    sub = lax.broadcasted_iota(jnp.int32, (8, LANES), 0)
    odd = lax.axis_index("plane") % 2
    active = [jnp.where(up, 0, T) + 8 * h + sub < length for h in range(2)]
    for r in range(N):
        for h in range(2):
            at = pl.ds(r * T + 8 * h, 8)
            c = [
                coupling[pl.ds(m * (N * T) + (r * T + 8 * h), 8), :]
                for m in (1 - odd, odd, 2, 3)
            ]
            own = here[at, :]
            value = residual[at, :] + (
                (c[0] * near[at, :] + c[1] * far[at, :])
                + (c[2] * pltpu.roll(own, 1, 1) + c[3] * pltpu.roll(own, LANES - 1, 1))
            )
            s_buf[at, :] = jnp.where(active[h], value, 0.0)

    index = jnp.broadcast_to(partner_ref[...], (8, LANES))
    facing = [jnp.take_along_axis(face[pl.ds(8 * h * 16, 8, stride=16), :], index, axis=1) for h in range(2)]
    weight = jnp.broadcast_to(flag_ref[...].astype(F32), (8, LANES)) * jnp.where(up, 1.0, 0.0)

    def at_level(t):
        lev = jnp.where(up, t, T - 1 - t)
        return [s_buf[pl.ds(lev + 8 * h * T, 8, stride=T), :] for h in range(2)]

    m = [spread(facing[w // 8], w % 8) for w in range(N)]
    y = at_level(0)
    for h in range(2):
        wake = total(k_buf[pl.ds(h * 8 * N + w, 8, stride=N), :] * m[w] for w in range(N))
        y[h] = y[h] - weight * wake
    for t in range(T):
        for h in range(2):
            y_ref[pl.ds(8 * h * T + t, 8, stride=T), :] = y[h]
        m = [spread(y[p // 8], p % 8) for p in range(N)]
        linked = jnp.where(up, t + 1, 2 * T - 1 - t) < length
        sums = [
            jnp.where(linked, total(g_ref[pl.ds(t * 256 + p * N + 8 * h, 8), :] * m[p] for p in range(N)), 0.0)
            for h in range(2)
        ]
        if t + 1 < T:
            y = [a - b for a, b in zip(at_level(t + 1), sums)]
        else:
            for h in range(2):
                q_ref[pl.ds(8 * h, 8), :] = sums[h]


def inner_kernel(u_ref, i_ref, g_ref, y_ref, x_ref, turned_ref):
    def turn(t, carry):
        for v in range(N):
            for h in range(2):
                column = g_ref[pl.ds(t * 256 + 8 * h * N + v, 8, stride=N), :]
                turned_ref[pl.ds(t * 256 + v * N + 8 * h, 8), :] = column
        return carry

    lax.fori_loop(0, T, turn, 0)
    for h in range(2):
        def u(p, v):
            return u_ref[pl.ds(h * 8 * 256 + p * N + v, 8, stride=256), :]

        def i(q, k):
            return i_ref[pl.ds(h * 8 * 24 + q * 3 + k, 8, stride=24), :]

        y = [y_ref[pl.ds(p * T + 8 * h, 8), :] for p in range(N)]
        z = [None] * N
        for q in range(N // 2):
            p0, p1 = 2 * q, 2 * q + 1
            for v in range(p1 + 1, N):
                y[v] = y[v] - (u(p0, v) * y[p0] + u(p1, v) * y[p1])
            i00, i01, i11 = i(q, 0), i(q, 1), i(q, 2)
            z[p0] = i00 * y[p0] + i01 * y[p1]
            z[p1] = i01 * y[p0] + i11 * y[p1]
        for q in reversed(range(N // 2)):
            for p in (2 * q, 2 * q + 1):
                for v in range(2 * q + 2, N):
                    z[p] = z[p] - u(p, v) * z[v]
        for p in range(N):
            x_ref[pl.ds(p * T + 8 * h, 8), :] = z[p]


def outer_kernel(
    s_ref, p_ref, turned_ref, x0_ref, y_ref, length_ref, q_ref, x_ref, inv_ref, w_buf, v_buf, u_buf, b_buf
):
    sub = lax.broadcasted_iota(jnp.int32, (8, LANES), 0)
    zero = jnp.zeros((8, LANES), F32)
    rows = [s_ref[pl.ds(r * 8, 8), :] + p_ref[pl.ds(r * 8, 8), :] for r in range(24)]
    lo, hi = rows[:8], rows[8:]
    eye = [jnp.where(sub == r, 1.0, 0.0) for r in range(8)]

    def u_put(p, low, high):
        if low is not None:
            u_buf[pl.ds(p * N, 8), :] = low
        u_buf[pl.ds(p * N + 8, 8), :] = high

    forward(lo, hi, eye + [zero] * 8, [zero] * 8 + eye, u_put, lambda q, v: None, w_buf, v_buf, b_buf)
    backward(u_buf, 0, v_buf, inv_ref, 0)
    up = going_up()
    length = jnp.broadcast_to(length_ref[...], (8, LANES))
    last = T - 1
    rhs = [y_ref[pl.ds(8 * h * T + last, 8, stride=T), :] - q_ref[pl.ds(8 * h, 8), :] for h in range(2)]
    m = [spread(rhs[p // 8], p % 8) for p in range(N)]
    x = [total(inv_ref[pl.ds(p * N + 8 * h, 8), :] * m[p] for p in range(N)) for h in range(2)]
    for t in reversed(range(T)):
        if t < last:
            m = [spread(x[v // 8], v % 8) for v in range(N)]
            x = [
                x0_ref[pl.ds(8 * h * T + t, 8, stride=T), :]
                - total(turned_ref[pl.ds(t * 256 + v * N + 8 * h, 8), :] * m[v] for v in range(N))
                for h in range(2)
            ]
        active = jnp.where(up, 0, 2 * T - 1 - t) < length
        x = [jnp.where(active, value, 0.0) for value in x]
        lev = jnp.where(up, t, last - t)
        for h in range(2):
            x_ref[pl.ds(lev + 8 * h * T, 8, stride=T), :] = x[h]


ANY = pl.BlockSpec(memory_space=pltpu.HBM)
LOCAL = pl.BlockSpec(memory_space=pltpu.VMEM)


def call(kernel, name, outs, ins, scratch, args, flops, limit=24):
    return pl.pallas_call(
        kernel,
        out_shape=tuple(
            jax.ShapeDtypeStruct(rows + (LANES,) if isinstance(rows, tuple) else (rows, LANES), F32)
            for rows in outs
        ),
        in_specs=ins,
        out_specs=[LOCAL] * len(outs),
        scratch_shapes=scratch,
        compiler_params=pltpu.CompilerParams(vmem_limit_bytes=limit * 2**20),
        cost_estimate=pl.CostEstimate(flops=flops, bytes_accessed=4 * 2**20, transcendentals=0),
        name=name,
    )(*args)


def factor(jacobian, line_length):
    block = pltpu.VMEM((N * N, LANES), F32)
    return call(
        factor_kernel,
        "factor",
        (T * 256, T * 256, T * 24, 192, 192, (N, N)),
        [ANY, ANY],
        [pltpu.VMEM((T, N, N, LANES), F32)] * 2
        + [block] * 5
        + [pltpu.VMEM((1, LANES), jnp.int32)]
        + [pltpu.SemaphoreType.DMA((T,))] * 2
        + [pltpu.SemaphoreType.DMA] * 2,
        (jacobian, line_length),
        10**10,
        48,
    )


def per_device(
    jacobian, residual, previous_update, offline_coupling, wake_partner, line_length, bottom_flag
):
    planes = lax.axis_size("plane")
    block = pltpu.VMEM((N * N, LANES), F32)
    here = previous_update.reshape(N * T, LANES)
    face = lax.ppermute(
        previous_update[:, :16].reshape(N * 16, LANES),
        ("wall", "plane"),
        [(i, (i + planes // 2) % planes) for i in range(planes)],
    )
    near = lax.ppermute(here, "plane", [(i, i ^ 1) for i in range(planes)])
    across = [(i, i + 1) for i in range(1, planes - 1, 2)]
    far = lax.ppermute(here, "plane", across + [(b, a) for a, b in across])
    g, u, i, s, p, k = factor(
        jacobian, pltpu.with_memory_space_constraint(line_length, pltpu.HBM)
    )
    swap = [(0, 1), (1, 0)]
    p = lax.ppermute(p, "wall", swap)
    y, q = call(
        source_kernel,
        "source",
        (256, 16),
        [LOCAL] * 11,
        [block],
        (
            k.reshape(N * N, LANES),
            residual.reshape(N * T, LANES),
            here,
            face,
            near,
            far,
            offline_coupling.reshape(4 * N * T, LANES),
            wake_partner,
            line_length,
            bottom_flag,
            g,
        ),
        10**9,
    )
    q = lax.ppermute(q, "wall", swap)
    x, turned = call(
        inner_kernel, "inner", (256, T * 256), [LOCAL] * 4, [], (u, i, g, y), 2 * 10**9
    )
    (update,) = call(
        outer_kernel,
        "outer",
        (256,),
        [LOCAL] * 7,
        [block] * 5,
        (s, p, turned, x, y, line_length, q),
        10**9,
    )
    return update.reshape(N, T, 1, LANES)


def solution(mesh):
    return jax.shard_map(
        per_device,
        mesh=mesh,
        in_specs=(
            P(None, None, None, "wall", "plane", None),
            P(None, "wall", "plane", None),
            P(None, "wall", "plane", None),
            P(None, None, "wall", "plane", None),
            P("plane", None),
            P("plane", None),
            P("plane", None),
        ),
        out_specs=P(None, "wall", "plane", None),
        check_vma=False,
    )
```

time: 37.7 us -> 29.5 us (0.78)
  the two profiles are of different devices: /device:TPU:6 before, /device:TPU:1 now
where the time goes in v2:
time: 29.5 us; the launch traced here: 29.3 us
  starting transfers between devices  18 us (61%)
  Pallas kernels  10.2 us (35%)
  waiting for transfers between devices  0.89 us (3%)
    pallas_call x4, Pallas kernels, call(): pl.pallas_call(kernel, out_shape=tuple((jax.ShapeDtypeStruct(rows + (LANE...  10.2 us
    ppermute x1, starting transfers between devices, per_device(): lax.ppermute(previous_update[:, :16].reshape(N * 16, LANES), ('wall', 'pl...  9.91 us
    ppermute x1, starting transfers between devices, per_device(): far = lax.ppermute(here, 'plane', across + [(b, a) for a, b in across])  6.42 us
    ppermute x1, starting transfers between devices, per_device(): q = lax.ppermute(q, 'wall', swap)  1.52 us
    ppermute x1, waiting for transfers between devices, per_device(): p = lax.ppermute(p, 'wall', swap)  0.7 us
  transfers between devices with their start and end apart: 5, of which 2 were waited for; matrix products, arithmetic and copies ran while one was open for 0% of the time, Pallas kernels for 31%

profile of v2, /device:TPU:1, one launch (start us, length us, event | category | flops | bytes accessed | tf_op | source)
XLA Modules:
  0.0 29.3 jit_solution(2769069075693279818)
XLA Ops:
  0.0 0.0 copy-start
  0.0 0.0 copy-start.1
  0.0 0.0 copy-start.2
  0.0 0.0 copy-start.3
  0.0 0.0 copy-start.4
  0.0 0.0 copy-start.5
  0.0 6.4 %collective-permute-start.3 = (f32[256,128]{1,0:T(8,128)}, f32[256,128]{1,0:T(8,128)S(1)}, u32[]{:S(2)}, u32[]{:S(2)}) collective-permute-start(f32[256,128]{1,0:T(8,128)} %bitcast.9), channel_id=1, source_target_pairs={{1,2},{3,4},{5,6},{7,8},{9,10},{11,12},{13,14},{15,16},{17,18},{19... | collective-permute-start | bytes 393224 | tf_op jit(solution)/shard_map/ppermute | solution.py:354
  6.5 0.1 collective-permute-start.2
  6.6 9.9 %collective-permute-start.1 = (f32[256,128]{1,0:T(8,128)}, f32[256,128]{1,0:T(8,128)S(1)}, u32[]{:S(2)}, u32[]{:S(2)}) collective-permute-start(f32[256,128]{1,0:T(8,128)} %bitcast.11), channel_id=1, source_target_pairs={{0,64},{1,65},{2,66},{3,67},{4,68},{5,69},{6,70},{7,71},{8,72},{9,... | collective-permute-start | bytes 393224 | tf_op jit(solution)/shard_map/ppermute | solution.py:347
  16.5 7.4 %factor.1 = (f32[4096,128]{1,0:T(8,128)S(1)}, f32[4096,128]{1,0:T(8,128)S(1)}, f32[384,128]{1,0:T(8,128)S(1)}, f32[192,128]{1,0:T(8,128)S(1)}, f32[192,128]{1,0:T(8,128)S(1)}, /*index=5*/f32[16,16,128]{2,1,0:T(8,128)S(1)}) custom-call(f32[3,16,16,16,1,128]{5,4,3,2,1,0:T(1,128)} %jac.1, s32[1,128]{1,0:T(1,128)} %length_ref.3), custom_call_target="tpu_custom_call" | custom-call | flops 10000000000 | bytes 4194304 | tf_op jit(solution)/shard_map/factor/pallas_call | solution.py:308
  23.9 0.1 collective-permute-start
  24.0 0.0 collective-permute-done.3.far
  24.0 0.0 collective-permute-done.2.near
  24.0 0.0 collective-permute-done.1.face
  24.0 0.0 copy-done
  24.0 0.0 copy-done.1
  24.0 0.0 copy-done.2
  24.0 0.0 copy-done.3
  24.0 0.0 copy-done.4
  24.0 0.0 copy-done.5
  24.1 0.4 %source.1 = (f32[256,128]{1,0:T(8,128)S(1)}, f32[16,128]{1,0:T(8,128)S(1)}) custom-call(f32[256,128]{1,0:T(8,128)S(1)} %bitcast.13, f32[256,128]{1,0:T(8,128)S(1)} %bitcast.8, f32[256,128]{1,0:T(8,128)S(1)} %bitcast.12, f32[256,128]{1,0:T(8,128)S(1)} %collective-permute-done.1.face, f32[256,128]{1,0:T(8,128)S(1)} %collective-permute-done.2.near, ...), custom_call_target="tpu_custom_call" | custom-call | flops 1000000000 | bytes 4194304 | tf_op jit(solution)/shard_map/source/pallas_call | solution.py:308
  24.5 1.5 %collective-permute-start.4 = (f32[16,128]{1,0:T(8,128)S(1)}, f32[16,128]{1,0:T(8,128)S(1)}, u32[]{:S(2)}, u32[]{:S(2)}) collective-permute-start(f32[16,128]{1,0:T(8,128)S(1)} %get-tuple-element.24), channel_id=1, source_target_pairs={{0,128},{128,0},{1,129},{129,1},{2,130},{130,2},{3,131},{131,3},{4... | collective-permute-start | bytes 24584 | tf_op jit(solution)/shard_map/ppermute | solution.py:381
  26.0 1.3 %inner.1 = (f32[256,128]{1,0:T(8,128)S(1)}, f32[4096,128]{1,0:T(8,128)S(1)}) custom-call(f32[4096,128]{1,0:T(8,128)S(1)} %get-tuple-element.17.u_ref, f32[384,128]{1,0:T(8,128)S(1)} %get-tuple-element.18.i_ref, f32[4096,128]{1,0:T(8,128)S(1)} %get-tuple-element.19.g_ref, f32[256,128]{1,0:T(8,128)S(1)} %get-tuple-element.21.y_ref), custom_call_target="tpu_custom_call" | custom-call | flops 2000000000 | bytes 4194304 | tf_op jit(solution)/shard_map/inner/pallas_call | solution.py:308
  27.3 0.7 %collective-permute-done.p_ref = f32[192,128]{1,0:T(8,128)S(1)} collective-permute-done((f32[192,128]{1,0:T(8,128)S(1)}, f32[192,128]{1,0:T(8,128)S(1)}, u32[]{:S(2)}, u32[]{:S(2)}) %collective-permute-start) | collective-permute-done | bytes 98336 | tf_op jit(solution)/shard_map/ppermute | solution.py:359
  28.0 0.2 collective-permute-done.4.q_ref
  28.2 1.1 %outer.1 = f32[256,128]{1,0:T(8,128)} custom-call(f32[192,128]{1,0:T(8,128)S(1)} %get-tuple-element.15.s_ref, f32[192,128]{1,0:T(8,128)S(1)} %collective-permute-done.p_ref, f32[4096,128]{1,0:T(8,128)S(1)} %get-tuple-element.22.turned_ref, f32[256,128]{1,0:T(8,128)S(1)} %get-tuple-element.23.x0_ref, f32[256,128]{1,0:T(8,128)S(1)} %get-tuple-element.21.y_ref, ...), custom_call_target="tpu_custom_call" | custom-call | flops 1000000000 | bytes 4194304 | tf_op jit(solution)/shard_map/outer/pallas_call | solution.py:308
Async XLA Ops:
  0.0 24.0 %copy-start = (f32[4,16,16,1,128]{4,3,2,1,0:T(1,128)S(1)}, f32[4,16,16,1,128]{4,3,2,1,0:T(1,128)}, u32[]{:S(2)}) copy-start(f32[4,16,16,1,128]{4,3,2,1,0:T(1,128)} %param.10) | copy-start | bytes 1572868
  0.0 24.0 %copy-start.1 = (f32[16,16,1,128]{3,2,1,0:T(1,128)S(1)}, f32[16,16,1,128]{3,2,1,0:T(1,128)}, u32[]{:S(2)}) copy-start(f32[16,16,1,128]{3,2,1,0:T(1,128)} %param.8) | copy-start | bytes 393220
  0.0 24.0 %copy-start.2 = (f32[16,16,1,128]{3,2,1,0:T(1,128)S(1)}, f32[16,16,1,128]{3,2,1,0:T(1,128)}, u32[]{:S(2)}) copy-start(f32[16,16,1,128]{3,2,1,0:T(1,128)} %param.9) | copy-start | bytes 393220
  0.0 24.0 %copy-start.3 = (s32[1,128]{1,0:T(1,128)S(1)}, s32[1,128]{1,0:T(1,128)}, u32[]{:S(2)}) copy-start(s32[1,128]{1,0:T(1,128)} %partner_ref.1) | copy-start | bytes 1540
  0.0 24.0 %copy-start.4 = (s32[1,128]{1,0:T(1,128)S(1)}, s32[1,128]{1,0:T(1,128)}, u32[]{:S(2)}) copy-start(s32[1,128]{1,0:T(1,128)} %flag_ref.1) | copy-start | bytes 1540
  0.0 24.0 %copy-start.5 = (s32[1,128]{1,0:T(1,128)S(1)}, s32[1,128]{1,0:T(1,128)}, u32[]{:S(2)}) copy-start(s32[1,128]{1,0:T(1,128)} %length_ref.3) | copy-start | bytes 1540
  0.0 23.9 %collective-permute-start.3 = (f32[256,128]{1,0:T(8,128)}, f32[256,128]{1,0:T(8,128)S(1)}, u32[]{:S(2)}, u32[]{:S(2)}) collective-permute-start(f32[256,128]{1,0:T(8,128)} %bitcast.9), channel_id=1, source_target_pairs={{1,2},{3,4},{5,6},{7,8},{9,10},{11,12},{13,14},{15,16},{17,18},{19... | collective-permute-start | bytes 393224 | tf_op jit(solution)/shard_map/ppermute | solution.py:354
  6.5 17.5 %collective-permute-start.2 = (f32[256,128]{1,0:T(8,128)}, f32[256,128]{1,0:T(8,128)S(1)}, u32[]{:S(2)}, u32[]{:S(2)}) collective-permute-start(f32[256,128]{1,0:T(8,128)} %bitcast.10), channel_id=1, source_target_pairs={{0,1},{1,0},{2,3},{3,2},{4,5},{5,4},{6,7},{7,6},{8,9},{9,8},{10,11... | collective-permute-start | bytes 393224 | tf_op jit(solution)/shard_map/ppermute | solution.py:352
  6.6 17.4 %collective-permute-start.1 = (f32[256,128]{1,0:T(8,128)}, f32[256,128]{1,0:T(8,128)S(1)}, u32[]{:S(2)}, u32[]{:S(2)}) collective-permute-start(f32[256,128]{1,0:T(8,128)} %bitcast.11), channel_id=1, source_target_pairs={{0,64},{1,65},{2,66},{3,67},{4,68},{5,69},{6,70},{7,71},{8,72},{9,... | collective-permute-start | bytes 393224 | tf_op jit(solution)/shard_map/ppermute | solution.py:347
  23.9 4.2 %collective-permute-start = (f32[192,128]{1,0:T(8,128)S(1)}, f32[192,128]{1,0:T(8,128)S(1)}, u32[]{:S(2)}, u32[]{:S(2)}) collective-permute-start(f32[192,128]{1,0:T(8,128)S(1)} %get-tuple-element.16), channel_id=1, source_target_pairs={{0,128},{128,0},{1,129},{129,1},{2,130},{130,2},{3,131},{131,3},{4... | collective-permute-start | bytes 294920 | tf_op jit(solution)/shard_map/ppermute | solution.py:359
  24.5 3.7 %collective-permute-start.4 = (f32[16,128]{1,0:T(8,128)S(1)}, f32[16,128]{1,0:T(8,128)S(1)}, u32[]{:S(2)}, u32[]{:S(2)}) collective-permute-start(f32[16,128]{1,0:T(8,128)S(1)} %get-tuple-element.24), channel_id=1, source_target_pairs={{0,128},{128,0},{1,129},{129,1},{2,130},{130,2},{3,131},{131,3},{4... | collective-permute-start | bytes 24584 | tf_op jit(solution)/shard_map/ppermute | solution.py:381

commit v3 on v2

--- a/solution.py
+++ b/solution.py
@@ -96,13 +96,20 @@
 
 
 AHEAD = 4
-
-
-def factor_kernel(
-    jac, length_hbm,
-    g_ref, u_ref, i_ref, s_ref, p_ref, k_ref,
-    m_buf, c_buf, w_a, v_a, w_b, v_b, b_ref, l_buf, m_sem, c_sem, k_sem, l_sem
-):
+EARLY = 6
+
+
+def is_early():
+    return lax.axis_index("plane") // 2 % 4 == 0
+
+
+def linked(t, length_ref):
+    return jnp.where(going_up(), t + 1, 2 * T - 1 - t) < jnp.broadcast_to(length_ref[...], (8, LANES))
+
+
+def eliminate(first, last, jac, l_buf, g_ref, u_ref, i_ref, s_ref, odd, buffers, at_step):
+    m_buf, c_buf, w_a, v_a, b_ref, m_sem, c_sem = buffers
+    w_b, v_b = odd
     up = going_up()
     side = jnp.where(up, 2, 0)
 
@@ -116,19 +123,6 @@
     def fetch(t):
         for copy in copies(t):
             copy.start()
-
-    length_copy = pltpu.make_async_copy(length_hbm, l_buf, l_sem)
-    length_copy.start()
-    for t in range(AHEAD):
-        fetch(t)
-    wake_copy = pltpu.make_async_copy(jac.at[0, :, :, 0, 0, :], k_ref, k_sem)
-    zero = jnp.zeros((8, LANES), F32)
-    w_b[...] = jnp.zeros(w_b.shape, F32)
-    v_b[...] = jnp.zeros(v_b.shape, F32)
-    length_copy.wait()
-
-    def linked(t):
-        return jnp.where(up, t + 1, 2 * T - 1 - t) < jnp.broadcast_to(l_buf[...], (8, LANES))
 
     def level(t, w_p, v_p, w_t, v_t):
         for copy in copies(t):
@@ -139,11 +133,12 @@
             hi.append(m_buf[t, r, 8:16, :])
             wlo.append(c_buf[t, r, 0:8, :])
             whi.append(c_buf[t, r, 8:16, :])
-        lo, hi = coupled(lo[:8], hi, w_p, v_p, linked(t - 1))
-        for r in range(N):
-            if r < 8:
-                s_ref[pl.ds(r * 8, 8), :] = lo[r]
-            s_ref[pl.ds(64 + r * 8, 8), :] = hi[r]
+        lo, hi = coupled(lo[:8], hi, w_p, v_p, linked(t - 1, l_buf))
+        if s_ref is not None:
+            for r in range(N):
+                if r < 8:
+                    s_ref[pl.ds(r * 8, 8), :] = lo[r]
+                s_ref[pl.ds(64 + r * 8, 8), :] = hi[r]
 
         def u_put(p, low, high):
             if low is not None:
@@ -158,28 +153,105 @@
         backward(u_ref, t * 256, v_t, g_ref, t * 256)
 
     def body(h, carry):
-        @pl.when(h < (T - AHEAD) // 2)
+        @pl.when(h < last - AHEAD // 2)
         def _():
             fetch(2 * h + AHEAD)
             fetch(2 * h + AHEAD + 1)
 
+        at_step(h)
+        level(2 * h, w_b, v_b, w_a, v_a)
+        level(2 * h + 1, w_a, v_a, w_b, v_b)
+        return carry
+
+    return fetch, lambda: lax.fori_loop(first, last, body, 0)
+
+
+def early_kernel(
+    jac, length_hbm, g_ref, u_ref, i_ref, w_ref, v_ref, m_buf, c_buf, w_a, v_a, b_ref, l_buf, m_sem, c_sem, l_sem
+):
+    @pl.when(is_early())
+    def _():
+        length_copy = pltpu.make_async_copy(length_hbm, l_buf, l_sem)
+        length_copy.start()
+        buffers = m_buf, c_buf, w_a, v_a, b_ref, m_sem, c_sem
+        fetch, run = eliminate(
+            0, EARLY, jac, l_buf, g_ref, u_ref, i_ref, None, (w_ref, v_ref), buffers, lambda h: None
+        )
+        for t in range(AHEAD):
+            fetch(t)
+        w_ref[...] = jnp.zeros(w_ref.shape, F32)
+        v_ref[...] = jnp.zeros(v_ref.shape, F32)
+        length_copy.wait()
+        run()
+
+
+def factor_kernel(
+    jac, length_hbm, g_in, u_in, i_in, w_in, v_in,
+    g_ref, u_ref, i_ref, s_ref, p_ref, k_ref,
+    m_buf, c_buf, w_a, v_a, b_ref, w_b, v_b, l_buf, m_sem, c_sem, k_sem, l_sem, e_sem
+):
+    early = is_early()
+    zero = jnp.zeros((8, LANES), F32)
+    length_copy = pltpu.make_async_copy(length_hbm, l_buf, l_sem)
+    wake_copy = pltpu.make_async_copy(jac.at[0, :, :, 0, 0, :], k_ref, k_sem)
+    state_copies = [
+        pltpu.make_async_copy(w_in, w_b, e_sem.at[0]),
+        pltpu.make_async_copy(v_in, v_b, e_sem.at[1]),
+    ]
+    done_copies = [
+        pltpu.make_async_copy(g_in, g_ref.at[pl.ds(0, EARLY * 512)], e_sem.at[2]),
+        pltpu.make_async_copy(u_in, u_ref.at[pl.ds(0, EARLY * 512)], e_sem.at[3]),
+        pltpu.make_async_copy(i_in, i_ref.at[pl.ds(0, EARLY * 48)], e_sem.at[4]),
+    ]
+
+    def at_step(h):
         @pl.when(h == (T - AHEAD) // 2)
         def _():
             wake_copy.start()
 
-        level(2 * h, w_b, v_b, w_a, v_a)
-        level(2 * h + 1, w_a, v_a, w_b, v_b)
-        return carry
-
-    lax.fori_loop(0, T // 2, body, 0)
-    lo, hi = coupled([zero] * 8, [zero] * N, w_b, v_b, linked(T - 1))
+    buffers = m_buf, c_buf, w_a, v_a, b_ref, m_sem, c_sem
+    first = jnp.where(early, EARLY, 0)
+    fetch, run = eliminate(
+        first, T // 2, jac, l_buf, g_ref, u_ref, i_ref, s_ref, (w_b, v_b), buffers, at_step
+    )
+    length_copy.start()
+
+    @pl.when(early)
+    def _():
+        for copy in state_copies:
+            copy.start()
+
+    for t in range(AHEAD):
+        fetch(2 * first + t)
+
+    @pl.when(early)
+    def _():
+        for copy in done_copies:
+            copy.start()
+        for copy in state_copies:
+            copy.wait()
+
+    @pl.when(jnp.logical_not(early))
+    def _():
+        w_b[...] = jnp.zeros(w_b.shape, F32)
+        v_b[...] = jnp.zeros(v_b.shape, F32)
+
+    length_copy.wait()
+    run()
+    lo, hi = coupled([zero] * 8, [zero] * N, w_b, v_b, linked(T - 1, l_buf))
     for r, row in enumerate(lo + hi):
         p_ref[pl.ds(r * 8, 8), :] = row
+
+    @pl.when(early)
+    def _():
+        for copy in done_copies:
+            copy.wait()
+
     wake_copy.wait()
 
 
 def source_kernel(
-    k_buf, residual, here, face, near, far, coupling, partner_ref, length_ref, flag_ref, g_ref,
+    k_buf, residual, here, far, near, face, coupling, partner_ref, length_ref, flag_ref, g_ref,
     y_ref, q_ref, s_buf
 ):
     up = going_up()
@@ -320,21 +392,40 @@
     )(*args)
 
 
-def factor(jacobian, line_length):
+def factor_early(jacobian, length):
+    block = pltpu.VMEM((N * N, LANES), F32)
+    return call(
+        early_kernel,
+        "early",
+        (EARLY * 512, EARLY * 512, EARLY * 48, 256, 256),
+        [ANY, ANY],
+        [pltpu.VMEM((2 * EARLY, N, N, LANES), F32)] * 2
+        + [block] * 3
+        + [pltpu.VMEM((1, LANES), jnp.int32)]
+        + [pltpu.SemaphoreType.DMA((2 * EARLY,))] * 2
+        + [pltpu.SemaphoreType.DMA],
+        (jacobian, length),
+        10**10,
+        46,
+    )
+
+
+def factor(jacobian, length, state):
     block = pltpu.VMEM((N * N, LANES), F32)
     return call(
         factor_kernel,
         "factor",
         (T * 256, T * 256, T * 24, 192, 192, (N, N)),
-        [ANY, ANY],
+        [ANY] * 7,
         [pltpu.VMEM((T, N, N, LANES), F32)] * 2
         + [block] * 5
         + [pltpu.VMEM((1, LANES), jnp.int32)]
         + [pltpu.SemaphoreType.DMA((T,))] * 2
-        + [pltpu.SemaphoreType.DMA] * 2,
-        (jacobian, line_length),
+        + [pltpu.SemaphoreType.DMA] * 2
+        + [pltpu.SemaphoreType.DMA((5,))],
+        (jacobian, length, *state),
         10**10,
-        48,
+        46,
     )
 
 
@@ -343,18 +434,19 @@
 ):
     planes = lax.axis_size("plane")
     block = pltpu.VMEM((N * N, LANES), F32)
-    here = previous_update.reshape(N * T, LANES)
+    length = pltpu.with_memory_space_constraint(line_length, pltpu.HBM)
+    state = factor_early(jacobian, length)
+    ready, *state = lax.optimization_barrier((previous_update, *state))
+    here = ready.reshape(N * T, LANES)
     face = lax.ppermute(
-        previous_update[:, :16].reshape(N * 16, LANES),
+        here,
         ("wall", "plane"),
         [(i, (i + planes // 2) % planes) for i in range(planes)],
     )
     near = lax.ppermute(here, "plane", [(i, i ^ 1) for i in range(planes)])
     across = [(i, i + 1) for i in range(1, planes - 1, 2)]
     far = lax.ppermute(here, "plane", across + [(b, a) for a, b in across])
-    g, u, i, s, p, k = factor(
-        jacobian, pltpu.with_memory_space_constraint(line_length, pltpu.HBM)
-    )
+    g, u, i, s, p, k = factor(jacobian, length, state)
     swap = [(0, 1), (1, 0)]
     p = lax.ppermute(p, "wall", swap)
     y, q = call(
@@ -367,9 +459,9 @@
             k.reshape(N * N, LANES),
             residual.reshape(N * T, LANES),
             here,
+            far,
+            near,
             face,
-            near,
-            far,
             offline_coupling.reshape(4 * N * T, LANES),
             wake_partner,
             line_length,

time: 29.5 us -> 26.3 us (0.89)
  the two profiles are of different devices: /device:TPU:1 before, /device:TPU:6 now
where the time goes in v3:
time: 26.3 us; the launch traced here: 26.1 us
  Pallas kernels  11.9 us (45%)
  starting transfers between devices  8.91 us (34%)
  waiting for transfers between devices  5.19 us (20%)
    pallas_call x5, Pallas kernels, call(): pl.pallas_call(kernel, out_shape=tuple((jax.ShapeDtypeStruct(rows + (LANE...  11.9 us
    ppermute x1, starting transfers between devices, per_device(): far = lax.ppermute(here, 'plane', across + [(b, a) for a, b in across])  5.62 us
    ppermute x1, starting transfers between devices, per_device(): lax.ppermute(here, ('wall', 'plane'), [(i, (i + planes // 2) % planes) fo...  3.02 us
    ppermute x1, waiting for transfers between devices, per_device(): lax.ppermute(here, ('wall', 'plane'), [(i, (i + planes // 2) % planes) fo...  2.51 us
    ppermute x1, waiting for transfers between devices, per_device(): q = lax.ppermute(q, 'wall', swap)  2.19 us
  transfers between devices with their start and end apart: 5, of which 4 were waited for; matrix products, arithmetic and copies ran while one was open for 0% of the time, Pallas kernels for 19%

profile of v3, /device:TPU:6, one launch (start us, length us, event | category | flops | bytes accessed | tf_op | source)
XLA Modules:
  0.0 26.1 jit_solution(13342834823871652477)
XLA Ops:
  0.0 0.0 copy-start.2
  0.0 5.7 %early.1 = (f32[3072,128]{1,0:T(8,128)S(1)}, f32[3072,128]{1,0:T(8,128)S(1)}, f32[288,128]{1,0:T(8,128)S(1)}, f32[256,128]{1,0:T(8,128)S(1)}, f32[256,128]{1,0:T(8,128)S(1)}) custom-call(f32[3,16,16,16,1,128]{5,4,3,2,1,0:T(1,128)} %jac.3, s32[1,128]{1,0:T(1,128)} %length_ref.3), custom_call_target="tpu_custom_call" | custom-call | flops 10000000000 | bytes 4194304 | tf_op jit(solution)/shard_map/early/pallas_call | solution.py:380
  5.7 0.0 copy-done.2
  5.7 0.0 copy-start
  5.8 0.0 copy-start.1
  5.8 0.0 copy-start.3
  5.8 0.0 copy-start.4
  5.8 0.0 copy-start.5
  5.8 5.6 %collective-permute-start.1 = (f32[256,128]{1,0:T(8,128)S(1)}, f32[256,128]{1,0:T(8,128)S(1)}, u32[]{:S(2)}, u32[]{:S(2)}) collective-permute-start(f32[256,128]{1,0:T(8,128)S(1)} %bitcast.9), channel_id=1, source_target_pairs={{1,2},{3,4},{5,6},{7,8},{9,10},{11,12},{13,14},{15,16},{17,18},{19... | collective-permute-start | bytes 393224 | tf_op jit(solution)/shard_map/ppermute | solution.py:448
  11.4 0.1 collective-permute-start.2
  11.5 3.0 %collective-permute-start.3 = (f32[256,128]{1,0:T(8,128)S(1)}, f32[256,128]{1,0:T(8,128)S(1)}, u32[]{:S(2)}, u32[]{:S(2)}) collective-permute-start(f32[256,128]{1,0:T(8,128)S(1)} %bitcast.11), channel_id=1, source_target_pairs={{0,64},{1,65},{2,66},{3,67},{4,68},{5,69},{6,70},{7,71},{8,72},{9,... | collective-permute-start | bytes 393224 | tf_op jit(solution)/shard_map/ppermute | solution.py:441
  14.6 3.3 %factor.1 = (f32[4096,128]{1,0:T(8,128)S(1)}, f32[4096,128]{1,0:T(8,128)S(1)}, f32[384,128]{1,0:T(8,128)S(1)}, f32[192,128]{1,0:T(8,128)S(1)}, f32[192,128]{1,0:T(8,128)S(1)}, /*index=5*/f32[16,16,128]{2,1,0:T(8,128)S(1)}) custom-call(f32[3,16,16,16,1,128]{5,4,3,2,1,0:T(1,128)} %jac.3, s32[1,128]{1,0:T(1,128)} %length_ref.3, ...), custom_call_target="tpu_custom_call" | custom-call | flops 10000000000 | bytes 4194304 | tf_op jit(solution)/shard_map/factor/pallas_call | solution.py:380
  17.8 0.1 collective-permute-start
  17.9 0.4 %collective-permute-done.1.far = f32[256,128]{1,0:T(8,128)S(1)} collective-permute-done((f32[256,128]{1,0:T(8,128)S(1)}, f32[256,128]{1,0:T(8,128)S(1)}, u32[]{:S(2)}, u32[]{:S(2)}) %collective-permute-start.1) | collective-permute-done | bytes 131104 | tf_op jit(solution)/shard_map/ppermute | solution.py:448
  18.3 0.0 collective-permute-done.2.near
  18.3 2.5 %collective-permute-done.3.face = f32[256,128]{1,0:T(8,128)S(1)} collective-permute-done((f32[256,128]{1,0:T(8,128)S(1)}, f32[256,128]{1,0:T(8,128)S(1)}, u32[]{:S(2)}, u32[]{:S(2)}) %collective-permute-start.3) | collective-permute-done | bytes 131104 | tf_op jit(solution)/shard_map/ppermute | solution.py:441
  20.8 0.0 copy-done
  20.8 0.0 copy-done.1
  20.8 0.0 copy-done.3
  20.8 0.0 copy-done.4
  20.8 0.0 copy-done.5
  20.8 0.4 %source.1 = (f32[256,128]{1,0:T(8,128)S(1)}, f32[16,128]{1,0:T(8,128)S(1)}) custom-call(f32[256,128]{1,0:T(8,128)S(1)} %bitcast.13, f32[256,128]{1,0:T(8,128)S(1)} %bitcast.8, f32[256,128]{1,0:T(8,128)S(1)} %bitcast.12, f32[256,128]{1,0:T(8,128)S(1)} %collective-permute-done.1.far, f32[256,128]{1,0:T(8,128)S(1)} %collective-permute-done.2.near, ...), custom_call_target="tpu_custom_call" | custom-call | flops 1000000000 | bytes 4194304 | tf_op jit(solution)/shard_map/source/pallas_call | solution.py:380
  21.3 0.1 collective-permute-start.4
  21.4 1.3 %inner.1 = (f32[256,128]{1,0:T(8,128)S(1)}, f32[4096,128]{1,0:T(8,128)S(1)}) custom-call(f32[4096,128]{1,0:T(8,128)S(1)} %get-tuple-element.38.u_ref, f32[384,128]{1,0:T(8,128)S(1)} %get-tuple-element.39.i_ref, f32[4096,128]{1,0:T(8,128)S(1)} %get-tuple-element.40.g_ref, f32[256,128]{1,0:T(8,128)S(1)} %get-tuple-element.43.y_ref), custom_call_target="tpu_custom_call" | custom-call | flops 2000000000 | bytes 4194304 | tf_op jit(solution)/shard_map/inner/pallas_call | solution.py:380
  22.7 0.1 collective-permute-done.p_ref
  22.8 2.2 %collective-permute-done.4.q_ref = f32[16,128]{1,0:T(8,128)S(1)} collective-permute-done((f32[16,128]{1,0:T(8,128)S(1)}, f32[16,128]{1,0:T(8,128)S(1)}, u32[]{:S(2)}, u32[]{:S(2)}) %collective-permute-start.4) | collective-permute-done | bytes 8224 | tf_op jit(solution)/shard_map/ppermute | solution.py:473
  25.0 1.1 %outer.1 = f32[256,128]{1,0:T(8,128)} custom-call(f32[192,128]{1,0:T(8,128)S(1)} %get-tuple-element.36.s_ref, f32[192,128]{1,0:T(8,128)S(1)} %collective-permute-done.p_ref, f32[4096,128]{1,0:T(8,128)S(1)} %get-tuple-element.44.turned_ref, f32[256,128]{1,0:T(8,128)S(1)} %get-tuple-element.45.x0_ref, f32[256,128]{1,0:T(8,128)S(1)} %get-tuple-element.43.y_ref, ...), custom_call_target="tpu_custom_call" | custom-call | flops 1000000000 | bytes 4194304 | tf_op jit(solution)/shard_map/outer/pallas_call | solution.py:380
Async XLA Ops:
  0.0 5.7 %copy-start.2 = (f32[16,16,1,128]{3,2,1,0:T(1,128)S(1)}, f32[16,16,1,128]{3,2,1,0:T(1,128)}, u32[]{:S(2)}) copy-start(f32[16,16,1,128]{3,2,1,0:T(1,128)} %param.9) | copy-start | bytes 393220
  5.7 15.1 %copy-start = (f32[4,16,16,1,128]{4,3,2,1,0:T(1,128)S(1)}, f32[4,16,16,1,128]{4,3,2,1,0:T(1,128)}, u32[]{:S(2)}) copy-start(f32[4,16,16,1,128]{4,3,2,1,0:T(1,128)} %param.10) | copy-start | bytes 1572868
  5.8 15.1 %copy-start.1 = (f32[16,16,1,128]{3,2,1,0:T(1,128)S(1)}, f32[16,16,1,128]{3,2,1,0:T(1,128)}, u32[]{:S(2)}) copy-start(f32[16,16,1,128]{3,2,1,0:T(1,128)} %param.8) | copy-start | bytes 393220
  5.8 15.1 %copy-start.3 = (s32[1,128]{1,0:T(1,128)S(1)}, s32[1,128]{1,0:T(1,128)}, u32[]{:S(2)}) copy-start(s32[1,128]{1,0:T(1,128)} %partner_ref.1) | copy-start | bytes 1540
  5.8 15.0 %copy-start.4 = (s32[1,128]{1,0:T(1,128)S(1)}, s32[1,128]{1,0:T(1,128)}, u32[]{:S(2)}) copy-start(s32[1,128]{1,0:T(1,128)} %flag_ref.1) | copy-start | bytes 1540
  5.8 15.0 %copy-start.5 = (s32[1,128]{1,0:T(1,128)S(1)}, s32[1,128]{1,0:T(1,128)}, u32[]{:S(2)}) copy-start(s32[1,128]{1,0:T(1,128)} %length_ref.3) | copy-start | bytes 1540
  5.8 12.5 %collective-permute-start.1 = (f32[256,128]{1,0:T(8,128)S(1)}, f32[256,128]{1,0:T(8,128)S(1)}, u32[]{:S(2)}, u32[]{:S(2)}) collective-permute-start(f32[256,128]{1,0:T(8,128)S(1)} %bitcast.9), channel_id=1, source_target_pairs={{1,2},{3,4},{5,6},{7,8},{9,10},{11,12},{13,14},{15,16},{17,18},{19... | collective-permute-start | bytes 393224 | tf_op jit(solution)/shard_map/ppermute | solution.py:448
  11.4 6.9 %collective-permute-start.2 = (f32[256,128]{1,0:T(8,128)S(1)}, f32[256,128]{1,0:T(8,128)S(1)}, u32[]{:S(2)}, u32[]{:S(2)}) collective-permute-start(f32[256,128]{1,0:T(8,128)S(1)} %bitcast.10), channel_id=1, source_target_pairs={{0,1},{1,0},{2,3},{3,2},{4,5},{5,4},{6,7},{7,6},{8,9},{9,8},{10,11... | collective-permute-start | bytes 393224 | tf_op jit(solution)/shard_map/ppermute | solution.py:446
  11.5 9.3 %collective-permute-start.3 = (f32[256,128]{1,0:T(8,128)S(1)}, f32[256,128]{1,0:T(8,128)S(1)}, u32[]{:S(2)}, u32[]{:S(2)}) collective-permute-start(f32[256,128]{1,0:T(8,128)S(1)} %bitcast.11), channel_id=1, source_target_pairs={{0,64},{1,65},{2,66},{3,67},{4,68},{5,69},{6,70},{7,71},{8,72},{9,... | collective-permute-start | bytes 393224 | tf_op jit(solution)/shard_map/ppermute | solution.py:441
  17.8 5.0 %collective-permute-start = (f32[192,128]{1,0:T(8,128)S(1)}, f32[192,128]{1,0:T(8,128)S(1)}, u32[]{:S(2)}, u32[]{:S(2)}) collective-permute-start(f32[192,128]{1,0:T(8,128)S(1)} %get-tuple-element.37), channel_id=1, source_target_pairs={{0,128},{128,0},{1,129},{129,1},{2,130},{130,2},{3,131},{131,3},{4... | collective-permute-start | bytes 294920 | tf_op jit(solution)/shard_map/ppermute | solution.py:451
  21.3 3.7 %collective-permute-start.4 = (f32[16,128]{1,0:T(8,128)S(1)}, f32[16,128]{1,0:T(8,128)S(1)}, u32[]{:S(2)}, u32[]{:S(2)}) collective-permute-start(f32[16,128]{1,0:T(8,128)S(1)} %get-tuple-element.46), channel_id=1, source_target_pairs={{0,128},{128,0},{1,129},{129,1},{2,130},{130,2},{3,131},{131,3},{4... | collective-permute-start | bytes 24584 | tf_op jit(solution)/shard_map/ppermute | solution.py:473

commit v4 on v3

--- a/solution.py
+++ b/solution.py
@@ -239,8 +239,13 @@
     length_copy.wait()
     run()
     lo, hi = coupled([zero] * 8, [zero] * N, w_b, v_b, linked(T - 1, l_buf))
-    for r, row in enumerate(lo + hi):
-        p_ref[pl.ds(r * 8, 8), :] = row
+    sub = lax.broadcasted_iota(jnp.int32, (8, LANES), 0)
+    corner = zero
+    for r in range(8):
+        p_ref[pl.ds(r * 8, 8), :] = jnp.where(sub >= r, lo[r], hi[8 + r])
+        p_ref[pl.ds(64 + r * 8, 8), :] = hi[r]
+        corner = jnp.where(sub == r, hi[8 + r], corner)
+    p_ref[pl.ds(128, 8), :] = corner
 
     @pl.when(early)
     def _():
@@ -340,7 +345,14 @@
 ):
     sub = lax.broadcasted_iota(jnp.int32, (8, LANES), 0)
     zero = jnp.zeros((8, LANES), F32)
-    rows = [s_ref[pl.ds(r * 8, 8), :] + p_ref[pl.ds(r * 8, 8), :] for r in range(24)]
+    corner = p_ref[pl.ds(128, 8), :]
+    rows = [p_ref[pl.ds(r * 8, 8), :] for r in range(16)]
+    turned = [p_ref[pl.ds(r, 8, stride=8), :] for r in range(8)]
+    first = [jnp.where(sub >= r, rows[r], turned[r]) for r in range(8)]
+    second = [
+        jnp.where(sub < r, rows[r], jnp.where(sub == r, corner, turned[r])) for r in range(8)
+    ]
+    rows = [s_ref[pl.ds(r * 8, 8), :] + row for r, row in enumerate(first + rows[8:] + second)]
     lo, hi = rows[:8], rows[8:]
     eye = [jnp.where(sub == r, 1.0, 0.0) for r in range(8)]
 
@@ -415,7 +427,7 @@
     return call(
         factor_kernel,
         "factor",
-        (T * 256, T * 256, T * 24, 192, 192, (N, N)),
+        (T * 256, T * 256, T * 24, 192, 136, (N, N)),
         [ANY] * 7,
         [pltpu.VMEM((T, N, N, LANES), F32)] * 2
         + [block] * 5

time: 26.3 us -> 26.3 us (level)
  transfers between devices with their start and end apart: 5 -> 5, of which waited for: 4 -> 3; matrix products, arithmetic and copies ran while one was open for 0% -> 0% of each run, Pallas kernels for 19% -> 19%
where the time goes in v4:
time: 26.3 us; the launch traced here: 26.2 us
  Pallas kernels  11.9 us (45%)
  starting transfers between devices  8.91 us (34%)
  waiting for transfers between devices  5.18 us (20%)
    pallas_call x5, Pallas kernels, call(): pl.pallas_call(kernel, out_shape=tuple((jax.ShapeDtypeStruct(rows + (LANE...  11.9 us
    ppermute x1, starting transfers between devices, per_device(): far = lax.ppermute(here, 'plane', across + [(b, a) for a, b in across])  5.62 us
    ppermute x1, starting transfers between devices, per_device(): lax.ppermute(here, ('wall', 'plane'), [(i, (i + planes // 2) % planes) fo...  3.02 us
    ppermute x1, waiting for transfers between devices, per_device(): lax.ppermute(here, ('wall', 'plane'), [(i, (i + planes // 2) % planes) fo...  2.51 us
    ppermute x1, waiting for transfers between devices, per_device(): q = lax.ppermute(q, 'wall', swap)  2.3 us
  transfers between devices with their start and end apart: 5, of which 3 were waited for; matrix products, arithmetic and copies ran while one was open for 0% of the time, Pallas kernels for 19%

profile of v4, /device:TPU:6, one launch (start us, length us, event | category | flops | bytes accessed | tf_op | source)
XLA Modules:
  0.0 26.2 jit_solution(10168764027883884295)
XLA Ops:
  0.0 0.0 copy-start.2
  0.0 5.7 %early.1 = (f32[3072,128]{1,0:T(8,128)S(1)}, f32[3072,128]{1,0:T(8,128)S(1)}, f32[288,128]{1,0:T(8,128)S(1)}, f32[256,128]{1,0:T(8,128)S(1)}, f32[256,128]{1,0:T(8,128)S(1)}) custom-call(f32[3,16,16,16,1,128]{5,4,3,2,1,0:T(1,128)} %jac.3, s32[1,128]{1,0:T(1,128)} %length_ref.3), custom_call_target="tpu_custom_call" | custom-call | flops 10000000000 | bytes 4194304 | tf_op jit(solution)/shard_map/early/pallas_call | solution.py:392
  5.7 0.0 copy-done.2
  5.7 0.0 copy-start
  5.8 0.0 copy-start.1
  5.8 0.0 copy-start.3
  5.8 0.0 copy-start.4
  5.8 0.0 copy-start.5
  5.8 5.6 %collective-permute-start.1 = (f32[256,128]{1,0:T(8,128)S(1)}, f32[256,128]{1,0:T(8,128)S(1)}, u32[]{:S(2)}, u32[]{:S(2)}) collective-permute-start(f32[256,128]{1,0:T(8,128)S(1)} %bitcast.9), channel_id=1, source_target_pairs={{1,2},{3,4},{5,6},{7,8},{9,10},{11,12},{13,14},{15,16},{17,18},{19... | collective-permute-start | bytes 393224 | tf_op jit(solution)/shard_map/ppermute | solution.py:460
  11.4 0.1 collective-permute-start.2
  11.5 3.0 %collective-permute-start.3 = (f32[256,128]{1,0:T(8,128)S(1)}, f32[256,128]{1,0:T(8,128)S(1)}, u32[]{:S(2)}, u32[]{:S(2)}) collective-permute-start(f32[256,128]{1,0:T(8,128)S(1)} %bitcast.11), channel_id=1, source_target_pairs={{0,64},{1,65},{2,66},{3,67},{4,68},{5,69},{6,70},{7,71},{8,72},{9,... | collective-permute-start | bytes 393224 | tf_op jit(solution)/shard_map/ppermute | solution.py:453
  14.6 3.3 %factor.1 = (f32[4096,128]{1,0:T(8,128)S(1)}, f32[4096,128]{1,0:T(8,128)S(1)}, f32[384,128]{1,0:T(8,128)S(1)}, f32[192,128]{1,0:T(8,128)S(1)}, f32[136,128]{1,0:T(8,128)S(1)}, /*index=5*/f32[16,16,128]{2,1,0:T(8,128)S(1)}) custom-call(f32[3,16,16,16,1,128]{5,4,3,2,1,0:T(1,128)} %jac.3, s32[1,128]{1,0:T(1,128)} %length_ref.3, ...), custom_call_target="tpu_custom_call" | custom-call | flops 10000000000 | bytes 4194304 | tf_op jit(solution)/shard_map/factor/pallas_call | solution.py:392
  17.8 0.1 collective-permute-start
  17.9 0.4 %collective-permute-done.1.far = f32[256,128]{1,0:T(8,128)S(1)} collective-permute-done((f32[256,128]{1,0:T(8,128)S(1)}, f32[256,128]{1,0:T(8,128)S(1)}, u32[]{:S(2)}, u32[]{:S(2)}) %collective-permute-start.1) | collective-permute-done | bytes 131104 | tf_op jit(solution)/shard_map/ppermute | solution.py:460
  18.3 0.0 collective-permute-done.2.near
  18.3 2.5 %collective-permute-done.3.face = f32[256,128]{1,0:T(8,128)S(1)} collective-permute-done((f32[256,128]{1,0:T(8,128)S(1)}, f32[256,128]{1,0:T(8,128)S(1)}, u32[]{:S(2)}, u32[]{:S(2)}) %collective-permute-start.3) | collective-permute-done | bytes 131104 | tf_op jit(solution)/shard_map/ppermute | solution.py:453
  20.8 0.0 copy-done
  20.8 0.0 copy-done.1
  20.8 0.0 copy-done.3
  20.8 0.0 copy-done.4
  20.8 0.0 copy-done.5
  20.8 0.4 %source.1 = (f32[256,128]{1,0:T(8,128)S(1)}, f32[16,128]{1,0:T(8,128)S(1)}) custom-call(f32[256,128]{1,0:T(8,128)S(1)} %bitcast.13, f32[256,128]{1,0:T(8,128)S(1)} %bitcast.8, f32[256,128]{1,0:T(8,128)S(1)} %bitcast.12, f32[256,128]{1,0:T(8,128)S(1)} %collective-permute-done.1.far, f32[256,128]{1,0:T(8,128)S(1)} %collective-permute-done.2.near, ...), custom_call_target="tpu_custom_call" | custom-call | flops 1000000000 | bytes 4194304 | tf_op jit(solution)/shard_map/source/pallas_call | solution.py:392
  21.3 0.1 collective-permute-start.4
  21.4 1.3 %inner.1 = (f32[256,128]{1,0:T(8,128)S(1)}, f32[4096,128]{1,0:T(8,128)S(1)}) custom-call(f32[4096,128]{1,0:T(8,128)S(1)} %get-tuple-element.38.u_ref, f32[384,128]{1,0:T(8,128)S(1)} %get-tuple-element.39.i_ref, f32[4096,128]{1,0:T(8,128)S(1)} %get-tuple-element.40.g_ref, f32[256,128]{1,0:T(8,128)S(1)} %get-tuple-element.43.y_ref), custom_call_target="tpu_custom_call" | custom-call | flops 2000000000 | bytes 4194304 | tf_op jit(solution)/shard_map/inner/pallas_call | solution.py:392
  22.7 0.0 collective-permute-done.p_ref
  22.7 2.3 %collective-permute-done.4.q_ref = f32[16,128]{1,0:T(8,128)S(1)} collective-permute-done((f32[16,128]{1,0:T(8,128)S(1)}, f32[16,128]{1,0:T(8,128)S(1)}, u32[]{:S(2)}, u32[]{:S(2)}) %collective-permute-start.4) | collective-permute-done | bytes 8224 | tf_op jit(solution)/shard_map/ppermute | solution.py:485
  25.0 1.1 %outer.1 = f32[256,128]{1,0:T(8,128)} custom-call(f32[192,128]{1,0:T(8,128)S(1)} %get-tuple-element.36.s_ref, f32[136,128]{1,0:T(8,128)S(1)} %collective-permute-done.p_ref, f32[4096,128]{1,0:T(8,128)S(1)} %get-tuple-element.44.turned_ref, f32[256,128]{1,0:T(8,128)S(1)} %get-tuple-element.45.x0_ref, f32[256,128]{1,0:T(8,128)S(1)} %get-tuple-element.43.y_ref, ...), custom_call_target="tpu_custom_call" | custom-call | flops 1000000000 | bytes 4194304 | tf_op jit(solution)/shard_map/outer/pallas_call | solution.py:392
Async XLA Ops:
  0.0 5.7 %copy-start.2 = (f32[16,16,1,128]{3,2,1,0:T(1,128)S(1)}, f32[16,16,1,128]{3,2,1,0:T(1,128)}, u32[]{:S(2)}) copy-start(f32[16,16,1,128]{3,2,1,0:T(1,128)} %param.9) | copy-start | bytes 393220
  5.7 15.1 %copy-start = (f32[4,16,16,1,128]{4,3,2,1,0:T(1,128)S(1)}, f32[4,16,16,1,128]{4,3,2,1,0:T(1,128)}, u32[]{:S(2)}) copy-start(f32[4,16,16,1,128]{4,3,2,1,0:T(1,128)} %param.10) | copy-start | bytes 1572868
  5.8 15.1 %copy-start.1 = (f32[16,16,1,128]{3,2,1,0:T(1,128)S(1)}, f32[16,16,1,128]{3,2,1,0:T(1,128)}, u32[]{:S(2)}) copy-start(f32[16,16,1,128]{3,2,1,0:T(1,128)} %param.8) | copy-start | bytes 393220
  5.8 15.1 %copy-start.3 = (s32[1,128]{1,0:T(1,128)S(1)}, s32[1,128]{1,0:T(1,128)}, u32[]{:S(2)}) copy-start(s32[1,128]{1,0:T(1,128)} %partner_ref.1) | copy-start | bytes 1540
  5.8 15.0 %copy-start.4 = (s32[1,128]{1,0:T(1,128)S(1)}, s32[1,128]{1,0:T(1,128)}, u32[]{:S(2)}) copy-start(s32[1,128]{1,0:T(1,128)} %flag_ref.1) | copy-start | bytes 1540
  5.8 15.0 %copy-start.5 = (s32[1,128]{1,0:T(1,128)S(1)}, s32[1,128]{1,0:T(1,128)}, u32[]{:S(2)}) copy-start(s32[1,128]{1,0:T(1,128)} %length_ref.3) | copy-start | bytes 1540
  5.8 12.5 %collective-permute-start.1 = (f32[256,128]{1,0:T(8,128)S(1)}, f32[256,128]{1,0:T(8,128)S(1)}, u32[]{:S(2)}, u32[]{:S(2)}) collective-permute-start(f32[256,128]{1,0:T(8,128)S(1)} %bitcast.9), channel_id=1, source_target_pairs={{1,2},{3,4},{5,6},{7,8},{9,10},{11,12},{13,14},{15,16},{17,18},{19... | collective-permute-start | bytes 393224 | tf_op jit(solution)/shard_map/ppermute | solution.py:460
  11.4 6.9 %collective-permute-start.2 = (f32[256,128]{1,0:T(8,128)S(1)}, f32[256,128]{1,0:T(8,128)S(1)}, u32[]{:S(2)}, u32[]{:S(2)}) collective-permute-start(f32[256,128]{1,0:T(8,128)S(1)} %bitcast.10), channel_id=1, source_target_pairs={{0,1},{1,0},{2,3},{3,2},{4,5},{5,4},{6,7},{7,6},{8,9},{9,8},{10,11... | collective-permute-start | bytes 393224 | tf_op jit(solution)/shard_map/ppermute | solution.py:458
  11.5 9.3 %collective-permute-start.3 = (f32[256,128]{1,0:T(8,128)S(1)}, f32[256,128]{1,0:T(8,128)S(1)}, u32[]{:S(2)}, u32[]{:S(2)}) collective-permute-start(f32[256,128]{1,0:T(8,128)S(1)} %bitcast.11), channel_id=1, source_target_pairs={{0,64},{1,65},{2,66},{3,67},{4,68},{5,69},{6,70},{7,71},{8,72},{9,... | collective-permute-start | bytes 393224 | tf_op jit(solution)/shard_map/ppermute | solution.py:453
  17.8 4.9 %collective-permute-start = (f32[136,128]{1,0:T(8,128)S(1)}, f32[136,128]{1,0:T(8,128)S(1)}, u32[]{:S(2)}, u32[]{:S(2)}) collective-permute-start(f32[136,128]{1,0:T(8,128)S(1)} %get-tuple-element.37), channel_id=1, source_target_pairs={{0,128},{128,0},{1,129},{129,1},{2,130},{130,2},{3,131},{131,3},{4... | collective-permute-start | bytes 208904 | tf_op jit(solution)/shard_map/ppermute | solution.py:463
  21.3 3.7 %collective-permute-start.4 = (f32[16,128]{1,0:T(8,128)S(1)}, f32[16,128]{1,0:T(8,128)S(1)}, u32[]{:S(2)}, u32[]{:S(2)}) collective-permute-start(f32[16,128]{1,0:T(8,128)S(1)} %get-tuple-element.46), channel_id=1, source_target_pairs={{0,128},{128,0},{1,129},{129,1},{2,130},{130,2},{3,131},{131,3},{4... | collective-permute-start | bytes 24584 | tf_op jit(solution)/shard_map/ppermute | solution.py:485
